TPU v7x, 512 devices: a whole 4x4x16 slice. The times are simulated.
512 devices in a mesh: ev: 64 (over z, x_lo, core), uni: 8 (over x_hi, y).
Axes of the slice: x: 4 (x_hi: 2, x_lo: 2; x = x_hi * 2 + x_lo), y: 4, z: 16, core: 2. Of those that a mesh axis runs over, the one named last changes fastest.
Arguments:
- responses: bfloat16 [64, 1048576], P(None, 'ev'), may hold values from -0.25 to 0.25
- event_bins: int32 [1048576], P('ev'), may hold values from 0 to 4095, as said below
- nominal_weight: bfloat16 [1048576], P('ev'), may hold values from 0.5 to 2
- throws: int32 [64, 1024], P(None, 'uni'), may hold values from -2 to 2
Outputs:
- spectra: float32 [4096, 1024], P('ev', 'uni')
- covariance: float32 [4096, 4096], P('uni', 'ev')
Inputs may be any that keep to these rules, and one draw needn't show every extreme that they name: `event_bins`: within the 16384 events of each device, in order, the bins never fall.
All inputs are finite; a program needn't handle non-finite values.
Results may differ from a plain program's by a relative error of at most 0.00042.
Values sent between devices are 32-bit elements; how exact they have to be, the bound alone decides.
A program may use at most 64 MiB of HBM per device.

v0:
```python
import jax
import jax.numpy as jnp
from jax import lax
from jax.sharding import PartitionSpec as P

UNIVERSES = 1024
BINS = 4096


def body(responses, event_bins, nominal_weight, throws):
    event_count = event_bins.shape[0]
    block_size = min(512, event_count)
    block_count = event_count // block_size
    group_width = throws.shape[1]
    knob_throws = throws.astype(jnp.bfloat16)
    tile_width = min(512, BINS)
    tile_count = BINS // tile_width
    per_bin = event_count * lax.axis_size("ev") // BINS
    cov_scale = 1.0 / (UNIVERSES * per_bin)
    contract_first = (((0,), (0,)), ((), ()))
    contract_last = (((1,), (1,)), ((), ()))

    def weigh_block(step_index, buffer):
        first_event = step_index * block_size
        response_slice = lax.dynamic_slice_in_dim(responses, first_event, block_size, 1)
        nominal_slice = lax.dynamic_slice_in_dim(nominal_weight, first_event, block_size, 0)
        log_weight = lax.dot_general(
            response_slice, knob_throws, contract_first, preferred_element_type=jnp.float32
        )
        block_weights = (nominal_slice.astype(jnp.float32)[:, None] * jnp.exp(log_weight)).astype(
            jnp.bfloat16
        )
        return lax.dynamic_update_slice_in_dim(buffer, block_weights, first_event, 0)

    weights = lax.fori_loop(
        0, block_count, weigh_block, jnp.zeros((event_count, group_width), jnp.bfloat16)
    )
    block_iota = lax.broadcasted_iota(jnp.int32, (block_size,), 0)
    hist_parts = []
    nominal_parts = []
    for tile_number in range(tile_count):
        tile_base = tile_number * tile_width
        lower = jnp.sum((event_bins < tile_base).astype(jnp.int32))
        upper = jnp.sum((event_bins < tile_base + tile_width).astype(jnp.int32))
        needed = (upper - lower + block_size - 1) // block_size
        tile_ids = tile_base + lax.broadcasted_iota(jnp.int32, (1, tile_width), 1)

        def fill_block(step_index, carry, lower=lower, tile_ids=tile_ids):
            totals, nominal_totals = carry
            wanted = lower + step_index * block_size
            clamped = jnp.minimum(wanted, event_count - block_size)
            bin_slice = lax.dynamic_slice_in_dim(event_bins, clamped, block_size, 0)
            weight_slice = lax.dynamic_slice_in_dim(weights, clamped, block_size, 0)
            nominal_slice = lax.dynamic_slice_in_dim(nominal_weight, clamped, block_size, 0)
            fresh = clamped + block_iota >= wanted
            onehot = ((bin_slice[:, None] == tile_ids) & fresh[:, None]).astype(jnp.bfloat16)
            totals = totals + lax.dot_general(
                onehot, weight_slice, contract_first, preferred_element_type=jnp.float32
            )
            nominal_totals = nominal_totals + jnp.dot(
                nominal_slice, onehot, preferred_element_type=jnp.float32
            )
            return (totals, nominal_totals)

        start_totals = jnp.zeros((tile_width, group_width), jnp.float32)
        start_nominal = jnp.zeros((tile_width,), jnp.float32)
        tile_hist, tile_nominal = lax.fori_loop(
            0, needed, fill_block, (start_totals, start_nominal)
        )
        hist_parts.append(tile_hist)
        nominal_parts.append(tile_nominal)
    totals = jnp.concatenate(hist_parts, axis=0)
    nominal_totals = jnp.concatenate(nominal_parts, axis=0)
    owned_hist, owned_nominal = (
        lax.psum_scatter(totals, "ev", scatter_dimension=0, tiled=True),
        lax.psum_scatter(nominal_totals, "ev", scatter_dimension=0, tiled=True),
    )
    deviation = owned_hist - owned_nominal[:, None]
    product = lax.dot_general(
        lax.all_gather(deviation, "ev", axis=0, tiled=True),
        deviation,
        contract_last,
        precision=lax.Precision.HIGHEST,
        preferred_element_type=jnp.float32,
    )
    partial_value = cov_scale * product
    covariance = lax.psum_scatter(partial_value, "uni", scatter_dimension=0, tiled=True)
    spectra = owned_hist / per_bin
    return (spectra, covariance)


def solution(mesh):
    in_specs = (P(None, "ev"), P("ev"), P("ev"), P(None, "uni"))
    out_specs = (P("ev", "uni"), P("uni", "ev"))
    return jax.shard_map(body, mesh=mesh, in_specs=in_specs, out_specs=out_specs, check_vma=False)
```

profile of v0, /device:TPU:32, one launch (start us, length us, event | category | flops | bytes accessed | tf_op | source)
XLA Modules:
  0.0 717.0 jit_solution(6385911824468318063)
XLA Ops:
  7.2 1.7 convert_reduce_fusion
  19.4 2.2 broadcast_in_dim.7
  21.6 79.0 %while.117 = (s32[]{:T(128)}, bf16[16384,128]{1,0:T(8,128)(2,1)}, bf16[16384]{0:T(1024)(128)(2,1)}, bf16[64,16384]{1,0:T(8,128)(2,1)}, bf16[64,128]{1,0:T(8,128)...) while((s32[]{:T(128)}, bf16[16384,128]{1,0:T(8,128)(2,1)}, bf16[16384]{0:T(1024)(128)(2,1)}, ...), condition=%wide.region_3.0_spmd, body=%wide.region_2.0_spmd.sunk | while | flops 8520198 | bytes 219279 | solution.py:35
  22.4 1.7 fusion.168
  24.8 1.7 fusion.168
  27.3 1.7 fusion.168
  29.8 1.7 fusion.168
  32.3 1.7 fusion.168
  34.7 1.7 fusion.168
  37.2 1.7 fusion.168
  39.7 1.7 fusion.168
  42.1 1.7 fusion.168
  44.6 1.7 fusion.168
  47.1 1.7 fusion.168
  49.6 1.7 fusion.168
  52.0 1.7 fusion.168
  54.5 1.7 fusion.168
  57.0 1.7 fusion.168
  59.4 1.7 fusion.168
  61.9 1.7 fusion.168
  64.4 1.7 fusion.168
  66.8 1.7 fusion.168
  69.3 1.7 fusion.168
  71.8 1.7 fusion.168
  74.2 1.7 fusion.168
  76.7 1.7 fusion.168
  79.2 1.7 fusion.168
  81.6 1.7 fusion.168
  84.1 1.7 fusion.168
  86.6 1.7 fusion.168
  89.1 1.7 fusion.168
  91.5 1.7 fusion.168
  94.0 1.7 fusion.168
  96.4 1.7 fusion.168
  98.9 1.7 fusion.168
  100.7 16.3 %while.119 = (s32[]{:T(128)}, f32[512,128]{1,0:T(8,128)S(1)}, f32[512]{0:T(512)S(1)}, s32[]{:T(128)}, s32[]{:T(128)}, /*index=5*/s32[16384]{0:T(1024)}, bf16[163...) while((s32[]{:T(128)}, f32[512,128]{1,0:T(8,128)S(1)}, ...), condition=%wide.region_8.9_spmd.clone, body=%wide.region_7.8_spmd.clone.sunk | while | flops 68749320 | bytes 684759 | solution.py:67
  117.0 16.9 %while.118 = (s32[]{:T(128)}, f32[512,128]{1,0:T(8,128)S(1)}, f32[512]{0:T(512)S(1)}, s32[]{:T(128)}, s32[]{:T(128)}, /*index=5*/s32[16384]{0:T(1024)}, bf16[163...) while((s32[]{:T(128)}, f32[512,128]{1,0:T(8,128)S(1)}, ...), condition=%wide.region_5.6_spmd.clone, body=%wide.region_4.5_spmd.clone.sunk | while | flops 68748808 | bytes 678615 | solution.py:67
  133.9 20.8 %while.120 = (s32[]{:T(128)}, f32[512,128]{1,0:T(8,128)S(1)}, f32[512]{0:T(512)S(1)}, s32[]{:T(128)}, s32[]{:T(128)}, /*index=5*/s32[16384]{0:T(1024)}, bf16[163...) while((s32[]{:T(128)}, f32[512,128]{1,0:T(8,128)S(1)}, ...), condition=%wide.region_11.12_spmd.clone, body=%wide.region_10.11_spmd.clone.sunk | while | flops 68749320 | bytes 684759 | solution.py:67
  154.8 20.8 %while.121 = (s32[]{:T(128)}, f32[512,128]{1,0:T(8,128)S(1)}, f32[512]{0:T(512)S(1)}, s32[]{:T(128)}, s32[]{:T(128)}, /*index=5*/s32[16384]{0:T(1024)}, bf16[163...) while((s32[]{:T(128)}, f32[512,128]{1,0:T(8,128)S(1)}, ...), condition=%wide.region_14.15_spmd.clone, body=%wide.region_13.14_spmd.clone.sunk | while | flops 68749320 | bytes 684759 | solution.py:67
  175.6 20.5 %while.122 = (s32[]{:T(128)}, f32[512,128]{1,0:T(8,128)S(1)}, f32[512]{0:T(512)S(1)}, s32[]{:T(128)}, s32[]{:T(128)}, /*index=5*/s32[16384]{0:T(1024)}, bf16[163...) while((s32[]{:T(128)}, f32[512,128]{1,0:T(8,128)S(1)}, ...), condition=%wide.region_17.18_spmd.clone, body=%wide.region_16.17_spmd.clone.sunk | while | flops 68749320 | bytes 684759 | solution.py:67
  196.8 16.7 %while.123 = (s32[]{:T(128)}, f32[512,128]{1,0:T(8,128)S(1)}, f32[512]{0:T(512)S(1)}, s32[]{:T(128)}, s32[]{:T(128)}, /*index=5*/s32[16384]{0:T(1024)}, bf16[163...) while((s32[]{:T(128)}, f32[512,128]{1,0:T(8,128)S(1)}, ...), condition=%wide.region_20.21_spmd.clone, body=%wide.region_19.20_spmd.clone.sunk | while | flops 68749320 | bytes 684759 | solution.py:67
  214.2 16.3 %while.124 = (s32[]{:T(128)}, f32[512,128]{1,0:T(8,128)S(1)}, f32[512]{0:T(512)S(1)}, s32[]{:T(128)}, s32[]{:T(128)}, /*index=5*/s32[16384]{0:T(1024)}, bf16[163...) while((s32[]{:T(128)}, f32[512,128]{1,0:T(8,128)S(1)}, ...), condition=%wide.region_23.24_spmd.clone, body=%wide.region_22.23_spmd.clone.sunk | while | flops 68749320 | bytes 684759 | solution.py:67
  231.2 20.7 %while.125 = (s32[]{:T(128)}, f32[512,128]{1,0:T(8,128)S(1)}, f32[512]{0:T(512)S(1)}, s32[]{:T(128)}, s32[]{:T(128)}, /*index=5*/s32[16384]{0:T(1024)}, bf16[163...) while((s32[]{:T(128)}, f32[512,128]{1,0:T(8,128)S(1)}, ...), condition=%wide.region_26.27_spmd.clone, body=%wide.region_25.26_spmd.clone.sunk | while | flops 68749320 | bytes 684759 | solution.py:67
  256.6 214.2 %all-reduce = f32[4096]{0:T(1024)S(1)} all-reduce(f32[4096]{0:T(1024)S(1)} %constant_dynamic-update-slice_fusion.9), channel_id=3, replica_groups=mesh['ev'=64,'uni'=8] {'ev'}, use_global_device_ids=true, to_apply=%region_28.29.clone | all-reduce | flops 4096 | bytes 32768
  470.8 21.2 %reduce-scatter.3.cloned.1.call-done = f32[64,128]{1,0:T(8,128)} async-done(((f32[4096,128]{1,0:T(8,128)}), f32[64,128]{1,0:T(8,128)}) %reduce-scatter.3.cloned.1.call-update) | async-done | bytes 32784 | tf_op jit(solution)/shard_map/reduce_scatter | solution.py:75
  493.6 127.5 %all-gather.2.cloned.1.call-done = f32[4096,128]{1,0:T(8,128)} async-done(((f32[64,128]{1,0:T(8,128)}), f32[4096,128]{1,0:T(8,128)}) %all-gather.2.cloned.1.call-update) | async-done | bytes 2097168 | tf_op jit(solution)/shard_map/all_gather | solution.py:80
  621.1 5.0 convolution_multiply_fusion
  626.1 84.4 %reduce-scatter.5.cloned.1.call-done = f32[512,64]{0,1:T(8,128)} async-done(((f32[4096,64]{0,1:T(8,128)}), f32[512,64]{0,1:T(8,128)}) %reduce-scatter.5.cloned.1.call-update) | async-done | bytes 131088 | tf_op jit(solution)/shard_map/reduce_scatter | solution.py:87
  (373 shorter events, 158.6 us)
Async XLA Ops:
  7.2 484.9 %reduce-scatter.3.cloned.1.call-start = ((), (), s32[]{:S(2)}) async-start(), calls=%async_computation.2 | async-start | bytes 2129920 | tf_op jit(solution)/shard_map/reduce_scatter | solution.py:75
  196.1 0.7 copy-start.1
  213.5 0.7 copy-start.3
  230.5 0.7 copy-start.5
  251.9 1.0 copy-start.2
  251.9 1.0 copy-start.4
  251.9 1.1 copy-start.6
  253.1 1.4 copy-start
  254.5 366.6 %all-gather.2.cloned.1.call-start = ((), (), s32[]{:S(2)}) async-start(), calls=%async_computation.3 | async-start | bytes 2129920 | tf_op jit(solution)/shard_map/all_gather | solution.py:80
  493.5 216.9 %reduce-scatter.5.cloned.1.call-start = ((), (), s32[]{:S(2)}) async-start(), calls=%async_computation.4 | async-start | bytes 1179648 | tf_op jit(solution)/shard_map/reduce_scatter | solution.py:87
Sparse Core Ops, SparseCore 0:
  254.6 237.4 reduce-scatter.2
  494.8 126.2 all-gather.1
  626.2 84.2 reduce-scatter.4
where the time goes:
time: 723 us; the launch traced here: 717 us
  waiting for transfers between devices  233 us (32%)
  blocking collectives  214 us (30%)
  matrix products  129 us (18%)
  local copies, waits for them, and re-layouts  64.2 us (9%)
  other arithmetic  28.9 us (4%)
  between operations  24.4 us (3%)
  loops' own time  23 us (3%)
    unnamed x1, blocking collectives  214 us
    all_gather x1, waiting for transfers between devices, body(): lax.all_gather(deviation, 'ev', axis=0, tiled=True)  127 us
    reduce_scatter x1, waiting for transfers between devices, body(): lax.psum_scatter(partial_value, 'uni', scatter_dimension=0, tiled=True)  84.4 us
    dot_general x36, matrix products, fill_block(): lax.dot_general(onehot, weight_slice, contract_first, preferred_element_t...  56 us
    dot_general x32, matrix products, weigh_block(): lax.dot_general(response_slice, knob_throws, contract_first, preferred_el...  54.9 us
    dynamic_slice x36, local copies, waits for them, and re-layouts, fill_block(): bin_slice = lax.dynamic_slice_in_dim(event_bins, clamped, block_size, 0)  28 us
    dynamic_slice x72, local copies, waits for them, and re-layouts, fill_block(): lax.dynamic_slice_in_dim(nominal_weight, clamped, block_size, 0)  28 us
    convert_element_type x32, other arithmetic, weigh_block(): nominal_slice.astype(jnp.float32)[:, None] * jnp.exp(log_weight)  24.1 us
  transfers between devices with their start and end apart: 3, of which 3 were waited for; matrix products, arithmetic and copies ran while one was open for 0% of the time, Pallas kernels for 0%

commit v1 on v0

v1 whole, which is shorter than its diff:
```python
import functools

import jax
import jax.numpy as jnp
from jax import lax
from jax.experimental import pallas as pl
from jax.experimental.pallas import tpu as pltpu
from jax.sharding import PartitionSpec as P

LANES = 128
QUARTER = 32
BLOCK_ROWS = 72
CHUNK = 512
MESH = pl.DeviceIdType.MESH
F32 = jnp.float32


def hist_kernel(edges, resp, bins, nominal, throws_t, out, acc, weights):
    tiles = acc.shape[0] - 1
    chunks = resp.shape[1] // CHUNK
    zero_tile = jnp.zeros(acc.shape[1:], F32)

    def clear(t, carry):
        acc[t] = zero_tile
        return carry

    lax.fori_loop(0, tiles + 1, clear, 0)
    knob_throws = throws_t[...]
    bin_iota = lax.broadcasted_iota(jnp.int32, (2 * LANES, CHUNK), 0)

    def add_window(tile, bin_row):
        onehot = jnp.where(bin_iota == bin_row - tile * LANES, 1.0, 0.0).astype(jnp.bfloat16)
        part = lax.dot_general(
            weights[...], onehot, (((1,), (1,)), ((), ())), preferred_element_type=F32
        )
        acc[tile] += part[:, :LANES]
        acc[tile + 1] += part[:, LANES:]

    def step(i, carry):
        at = pl.ds(pl.multiple_of(i * CHUNK, CHUNK), CHUNK)
        nominal_row = nominal[:, at]
        log_weight = jnp.dot(knob_throws, resp[:, at], preferred_element_type=F32)
        weights[: 4 * QUARTER] = (nominal_row * jnp.exp(log_weight)).astype(jnp.bfloat16)
        weights[4 * QUARTER :] = jnp.broadcast_to(nominal_row, (16, CHUNK)).astype(jnp.bfloat16)
        bin_row = bins[:, at]
        first = edges[i, 0] // LANES
        last = edges[i, 1] // LANES
        add_window(first, bin_row)

        def more(w, c):
            add_window(first + 2 * w, bins[:, at])
            return c

        lax.fori_loop(1, (last - first) // 2 + 1, more, 0)
        return carry

    lax.fori_loop(0, chunks, step, 0)

    def arrange(zb, carry):
        for half in range(2):
            tile = acc[2 * zb + half]
            for quarter in range(4):
                dest = out.at[quarter % 2, zb, quarter // 2]
                dest[half * QUARTER : (half + 1) * QUARTER] = tile[
                    quarter * QUARTER : (quarter + 1) * QUARTER
                ]
        low = acc[2 * zb, 4 * QUARTER : 4 * QUARTER + 8]
        high = acc[2 * zb + 1, 4 * QUARTER : 4 * QUARTER + 8]
        row = lax.broadcasted_iota(jnp.int32, (8, LANES), 0)
        both = jnp.where(row == 0, low, high)
        for quarter in range(4):
            out[quarter % 2, zb, quarter // 2, 2 * QUARTER :] = both
        return carry

    lax.fori_loop(0, tiles // 2, arrange, 0)


def histogram(responses, event_bins, nominal_weight, throws, bins_total):
    events = event_bins.shape[0]
    tiles = bins_total // LANES
    by_chunk = event_bins.reshape(events // CHUNK, CHUNK)
    edges = jnp.stack([by_chunk[:, 0], by_chunk[:, -1]], axis=1)
    vmem = pl.BlockSpec(memory_space=pltpu.VMEM)
    return pl.pallas_call(
        hist_kernel,
        out_shape=jax.ShapeDtypeStruct((2, tiles // 2, 2, BLOCK_ROWS, LANES), F32),
        in_specs=[pl.BlockSpec(memory_space=pltpu.SMEM)] + [vmem] * 4,
        out_specs=vmem,
        scratch_shapes=[
            pltpu.VMEM((tiles + 1, 4 * QUARTER + 16, LANES), F32),
            pltpu.VMEM((4 * QUARTER + 16, CHUNK), jnp.bfloat16),
        ],
        name="histogram",
    )(
        edges,
        responses,
        event_bins.reshape(1, events),
        nominal_weight.astype(F32).reshape(1, events),
        throws.astype(jnp.bfloat16).T,
    )


def exchange_kernel(
    nz, nu, spec_scale, cov_scale,
    part, spectra, cov,
    core_in, summed, x_in, up_in, down_in, up_out, down_out, own, dev, up_blk, down_blk,
    rows_in, cols_in, spec_in, cols_mix, part_out, part_keep, part_in, pack_out, pack_in,
    core_s, core_r, x_s, x_r, up_s, up_r, down_s, down_r,
    gu_s, gu_r, gd_s, gd_r, fwd_s, rows_r, cols_s, cols_r, spec_s, spec_r, tail_s, tail_r,
):
    ev = lax.axis_index("ev")
    u = lax.axis_index("uni")
    z = ev // 4
    xl = lax.rem(ev // 2, 2)
    c = lax.rem(ev, 2)
    core_ev = ev + 1 - 2 * c
    x_ev = ev + 2 - 4 * xl
    diag_ev = x_ev + 1 - 2 * c
    up_ev = lax.rem(ev + 4, 4 * nz)
    down_ev = lax.rem(ev + 4 * nz - 4, 4 * nz)
    half = nz // 2

    def send(src, dst, ssem, rsem, to_ev=ev, to_u=u):
        return pltpu.make_async_remote_copy(
            src_ref=src, dst_ref=dst, send_sem=ssem, recv_sem=rsem,
            device_id={"ev": to_ev, "uni": to_u}, device_id_type=MESH,
        )

    def block_of(k):
        j = (k + 1) // 2
        away = jnp.where(lax.rem(k, 2) == 1, half - j, nz - half + j)
        return lax.rem(z + away, nz)

    barrier = pltpu.get_barrier_semaphore()
    for peer in (core_ev, x_ev, diag_ev, up_ev, down_ev):
        pl.semaphore_signal(barrier, inc=1, device_id={"ev": peer, "uni": u}, device_id_type=MESH)
    for j in range(1, nu):
        pl.semaphore_signal(
            barrier, inc=1, device_id={"ev": ev, "uni": lax.rem(u + j, nu)}, device_id_type=MESH
        )
    pl.semaphore_wait(barrier, 5 + nu - 1)

    def core_copy(k):
        zb = block_of(k)
        return send(part.at[1 - c, zb], core_in.at[zb], core_s.at[k], core_r.at[k], to_ev=core_ev)

    def x_copy(k):
        zb = block_of(k)
        return send(summed.at[zb, 1 - xl], x_in.at[zb], x_s.at[k], x_r.at[k], to_ev=x_ev)

    def start_core(k, carry):
        core_copy(k).start()
        return carry

    lax.fori_loop(0, nz, start_core, 0)

    def start_x(k, carry):
        zb = block_of(k)
        core_copy(k).wait_recv()
        summed[zb] = part[c, zb] + core_in[zb]
        x_copy(k).start()
        return carry

    lax.fori_loop(0, nz, start_x, 0)

    def up_copy(s):
        return send(up_out.at[s], up_in.at[s], up_s.at[s], up_r.at[s], to_ev=up_ev)

    def down_copy(s):
        return send(down_out.at[s], down_in.at[s], down_s.at[s], down_r.at[s], to_ev=down_ev)

    def local_sum(k):
        zb = block_of(k)
        x_copy(k).wait_recv()
        return summed[zb, xl] + x_in[zb]

    up_out[0] = local_sum(0)
    up_copy(0).start()
    down_out[0] = local_sum(2)
    down_copy(0).start()

    def ring_step(s, carry):
        here = local_sum(2 * s - 1)
        up_copy(s - 1).wait_recv()
        up_out[s] = here + up_in[s - 1]
        up_copy(s).start()

        @pl.when(s < half - 1)
        def _():
            here = local_sum(2 * s + 2)
            down_copy(s - 1).wait_recv()
            down_out[s] = here + down_in[s - 1]
            down_copy(s).start()

        return carry

    lax.fori_loop(1, half, ring_step, 0)
    here = local_sum(nz - 1)
    down_copy(half - 2).wait_recv()
    here = here + down_in[half - 2]
    up_copy(half - 1).wait_recv()
    total = here + up_in[half - 1]
    own[...] = total
    dev[:QUARTER] = total[:QUARTER] - total[2 * QUARTER : 2 * QUARTER + 1]
    dev[QUARTER:] = total[QUARTER : 2 * QUARTER] - total[2 * QUARTER + 1 : 2 * QUARTER + 2]

    def gather_up(s, src):
        return send(src, up_blk.at[s], gu_s.at[s], gu_r.at[s], to_ev=up_ev)

    def gather_down(s, src):
        return send(src, down_blk.at[s], gd_s.at[s], gd_r.at[s], to_ev=down_ev)

    def forward(n, src, origin, waiting=False):
        owner = origin // (nz // nu)
        slot = lax.rem(origin, nz // nu)

        @pl.when(owner != u)
        def _():
            copy = send(src, rows_in.at[slot, u], fwd_s.at[n], rows_r.at[slot, u], to_u=owner)
            if waiting:
                copy.wait_send()
            else:
                copy.start()

        if not waiting:

            @pl.when(owner == u)
            def _():
                rows_in[slot, u] = src[...]

    gather_up(0, dev).start()
    gather_down(0, dev).start()

    def cols_copy(j):
        return send(dev, cols_in.at[u], cols_s.at[j], cols_r.at[u], to_u=lax.rem(u + j, nu))

    def start_cols(j, carry):
        cols_copy(j).start()
        return carry

    forward(0, dev, z)
    lax.fori_loop(1, nu, start_cols, 0)
    cols_in[u] = dev[...]

    mine = 2 * xl + c
    spec_peers = ((core_ev, xl), (x_ev, 1 - xl), (diag_ev, 1 - xl))

    def spec_copy(i):
        peer, peer_half = spec_peers[i]
        src = own.at[pl.ds(pl.multiple_of(peer_half * QUARTER, QUARTER), QUARTER)]
        return send(src, spec_in.at[mine], spec_s.at[i], spec_r.at[i], to_ev=peer)

    for i in range(3):
        spec_copy(i).start()
    spec_in[mine] = own[pl.ds(pl.multiple_of(xl * QUARTER, QUARTER), QUARTER)]

    def gather_step(s, carry):
        gather_up(s, dev).wait_recv()

        @pl.when(s < half - 1)
        def _():
            gather_up(s + 1, up_blk.at[s]).start()

        forward(1 + 2 * s, up_blk.at[s], lax.rem(z + nz - 1 - s, nz))

        @pl.when(s < half - 1)
        def _():
            gather_down(s, dev).wait_recv()

            @pl.when(s < half - 2)
            def _():
                gather_down(s + 1, down_blk.at[s]).start()

            forward(2 + 2 * s, down_blk.at[s], lax.rem(z + 1 + s, nz))

        return carry

    lax.fori_loop(0, half, gather_step, 0)

    for i in range(3):
        spec_copy(i).wait_recv()
    by_bin = spec_in[...].reshape(4 * QUARTER, LANES).T
    spectra[...] = jnp.where(c == 0, by_bin[: LANES // 2], by_bin[LANES // 2 :]) * spec_scale

    def wait_cols(j, carry):
        v = lax.rem(u + j, nu)
        send(dev, cols_in.at[v], cols_s.at[j], cols_r.at[v], to_u=v).wait_recv()
        return carry

    lax.fori_loop(1, nu, wait_cols, 0)

    depth = nu * QUARTER
    lane = lax.broadcasted_iota(jnp.int32, (depth, LANES), 1)
    left = cols_in[:, :QUARTER].reshape(depth, LANES)
    right = cols_in[:, QUARTER:].reshape(depth, LANES)
    first = jnp.where(lane < LANES // 2, left, pltpu.roll(right, LANES // 2, 1))
    second = jnp.where(lane < LANES // 2, pltpu.roll(left, LANES // 2, 1), right)
    cols_mix[0] = first
    cols_mix[1] = second

    def wait_rows(j, carry):
        v = lax.rem(u + j, nu)
        for slot in range(nz // nu):
            send(dev, rows_in.at[slot, v], cols_s.at[0], rows_r.at[slot, v], to_u=v).wait_recv()
        return carry

    lax.fori_loop(1, nu, wait_rows, 0)

    def product(which, dest):
        cols = cols_mix[which]
        for slot in range(nz // nu):
            for h in range(2):
                rows = rows_in[slot, :, h * QUARTER : (h + 1) * QUARTER].reshape(depth, LANES)
                at = (2 * slot + h) * LANES
                dest[at : at + LANES] = jnp.dot(
                    rows.T, cols, precision=lax.Precision.HIGHEST, preferred_element_type=F32
                )

    product(1 - c, part_out)
    core_tail = send(part_out, part_in, tail_s.at[0], tail_r.at[0], to_ev=core_ev)
    core_tail.start()
    product(c, part_keep)
    core_tail.wait_recv()
    both = part_keep[...] + part_in[...]
    n_rows = both.shape[0] // 2
    lane = lax.broadcasted_iota(jnp.int32, (n_rows, LANES), 1)
    top, bottom = both[:n_rows], both[n_rows:]
    pack_left = jnp.where(lane < LANES // 2, top, pltpu.roll(bottom, LANES // 2, 1))
    pack_right = jnp.where(lane < LANES // 2, pltpu.roll(top, LANES // 2, 1), bottom)
    pack_out[...] = jnp.where(xl == 0, pack_right, pack_left)
    x_tail = send(pack_out, pack_in, tail_s.at[1], tail_r.at[1], to_ev=x_ev)
    x_tail.start()
    keep = jnp.where(xl == 0, pack_left, pack_right)
    x_tail.wait_recv()
    final = (keep + pack_in[...]) * cov_scale
    cov[:n_rows] = final[:, : LANES // 2]
    cov[n_rows:] = final[:, LANES // 2 :]

    def drain(k, carry):
        core_copy(k).wait_send()
        x_copy(k).wait_send()
        return carry

    lax.fori_loop(0, nz, drain, 0)

    def drain_ring(s, carry):
        up_copy(s).wait_send()
        gather_up(s, dev).wait_send()
        forward(1 + 2 * s, dev, lax.rem(z + nz - 1 - s, nz), waiting=True)

        @pl.when(s < half - 1)
        def _():
            down_copy(s).wait_send()
            gather_down(s, dev).wait_send()
            forward(2 + 2 * s, dev, lax.rem(z + 1 + s, nz), waiting=True)

        return carry

    lax.fori_loop(0, half, drain_ring, 0)
    forward(0, dev, z, waiting=True)

    def drain_cols(j, carry):
        cols_copy(j).wait_send()
        return carry

    lax.fori_loop(1, nu, drain_cols, 0)
    for i in range(3):
        spec_copy(i).wait_send()
    core_tail.wait_send()
    x_tail.wait_send()


def exchange(part, nz, nu, spec_scale, cov_scale):
    half = nz // 2
    rows = nz // nu * 2 * LANES
    block = (BLOCK_ROWS, LANES)
    blk = (2 * QUARTER, LANES)
    vmem = pl.BlockSpec(memory_space=pltpu.VMEM)

    def buf(*shape):
        return pltpu.VMEM(shape, F32)

    def dma(*shape):
        return pltpu.SemaphoreType.DMA(shape)

    return pl.pallas_call(
        functools.partial(exchange_kernel, nz, nu, spec_scale, cov_scale),
        out_shape=(
            jax.ShapeDtypeStruct((LANES // 2, 4 * QUARTER), F32),
            jax.ShapeDtypeStruct((rows, LANES // 2), F32),
        ),
        in_specs=[vmem],
        out_specs=(vmem, vmem),
        scratch_shapes=[
            buf(nz, 2, *block),
            buf(nz, 2, *block),
            buf(nz, *block),
            buf(half, *block), buf(half - 1, *block),
            buf(half, *block), buf(half - 1, *block),
            buf(*block), buf(*blk),
            buf(half, *blk), buf(half - 1, *blk),
            buf(nz // nu, nu, *blk), buf(nu, *blk),
            buf(4, QUARTER, LANES),
            buf(2, nu * QUARTER, LANES),
            buf(rows, LANES), buf(rows, LANES), buf(rows, LANES),
            buf(rows // 2, LANES), buf(rows // 2, LANES),
            dma(nz), dma(nz), dma(nz), dma(nz),
            dma(half), dma(half), dma(half - 1), dma(half - 1),
            dma(half), dma(half), dma(half - 1), dma(half - 1),
            dma(nz), dma(nz // nu, nu), dma(nu), dma(nu),
            dma(3), dma(3), dma(2), dma(2),
        ],
        compiler_params=pltpu.CompilerParams(collective_id=0, has_side_effects=True),
        name="exchange",
    )(part)


def body(responses, event_bins, nominal_weight, throws):
    nz = lax.axis_size("ev") // 4
    nu = lax.axis_size("uni")
    bins_total = nz * 2 * LANES
    per_bin = event_bins.shape[0] * lax.axis_size("ev") // bins_total
    universes = throws.shape[1] * nu
    part = histogram(responses, event_bins, nominal_weight, throws, bins_total)
    return exchange(part, nz, nu, 1.0 / per_bin, 1.0 / (universes * per_bin))


def solution(mesh):
    in_specs = (P(None, "ev"), P("ev"), P("ev"), P(None, "uni"))
    out_specs = (P("ev", "uni"), P("uni", "ev"))
    return jax.shard_map(body, mesh=mesh, in_specs=in_specs, out_specs=out_specs, check_vma=False)
```

time: 723 us -> 106 us (0.15)
  the two profiles are of different devices: /device:TPU:32 before, /device:TPU:5 now
where the time goes in v1:
time: 106 us; the launch traced here: 105 us
  Pallas kernels  97 us (92%)
  local copies, waits for them, and re-layouts  4.74 us (4%)
  other arithmetic  2.83 us (3%)
    pallas_call x1, Pallas kernels, exchange(): pl.pallas_call(functools.partial(exchange_kernel, nz, nu, spec_scale, cov...  82.4 us
    pallas_call x1, Pallas kernels, histogram(): pl.pallas_call(hist_kernel, out_shape=jax.ShapeDtypeStruct((2, tiles // 2...  14.7 us

profile of v1, /device:TPU:5, one launch (start us, length us, event | category | flops | bytes accessed | tf_op | source)
XLA Modules:
  0.0 105.3 jit_solution(379120724291263971)
XLA Ops:
  0.6 0.8 convert_element_type.4
  1.4 0.7 copy.18
  2.1 1.4 %reshape.19 = f32[16384]{0:T(1024)} convert(bf16[16384]{0:T(1024)(128)(2,1)} %param.6) | non-fusion elementwise | flops 16384 | bytes 98304 | tf_op jit(solution)/shard_map/reshape | solution.py:98
  3.5 0.9 reshape.15
  4.4 0.1 fusion
  4.4 0.7 pad_add_fusion.edges
  5.1 14.7 %histogram.1.part = f32[2,16,2,72,128]{4,3,2,1,0:T(8,128)} custom-call(s32[32,2]{1,0:T(8,128)} %pad_add_fusion.edges, bf16[64,16384]{1,0:T(8,128)(2,1)} %resp.1, s32[1,16384]{1,0:T(1,128)} %bitcast.3, f32[1,16384]{1,0:T(1,128)} %bitcast.4, bf16[128,64]{1,0:T(8,128)(2,1)} %bitcast.5), custom_call_target="tpu_custom_call" | custom-call | tf_op jit(solution)/shard_map/histogram/pallas_call | solution.py:84
  19.8 82.4 %exchange.1 = (f32[64,128]{1,0:T(8,128)}, f32[512,64]{1,0:T(8,128)}) custom-call(f32[2,16,2,72,128]{4,3,2,1,0:T(8,128)} %histogram.1.part), custom_call_target="tpu_custom_call" | custom-call | tf_op jit(solution)/shard_map/exchange/pallas_call | solution.py:386
  102.2 1.7 %copy.19 = f32[512,64]{0,1:T(8,128)} copy(f32[512,64]{1,0:T(8,128)} %get-tuple-element.11) | data formatting | bytes 262144 | tf_op jit(solution)/shard_map/exchange/pallas_call | solution.py:386
  103.9 1.4 %copy.21 = f32[64,128]{1,0:T(8,128)} copy(f32[64,128]{1,0:T(8,128)} %get-tuple-element.16) | data formatting | bytes 65536

commit v2 on v1

v2 whole, which is shorter than its diff:
```python
import functools

import jax
import jax.numpy as jnp
from jax import lax
from jax.experimental import pallas as pl
from jax.experimental.pallas import tpu as pltpu
from jax.sharding import PartitionSpec as P

LANES = 128
QUARTER = 32
BLOCK_ROWS = 72
CHUNK = 512
VMEM_GRANT = 20 << 20
MESH = pl.DeviceIdType.MESH
F32 = jnp.float32


def hist_kernel(
    resp_hbm, bins_hbm, nominal_hbm, throws_hbm,
    out,
    acc, weights, nominal_rows, resp, bins, nominal, throws, edges, sems,
):
    copies = [
        pltpu.make_async_copy(src, dst, sems.at[i])
        for i, (src, dst) in enumerate(
            [
                (throws_hbm, throws), (bins_hbm, edges), (nominal_hbm, nominal),
                (bins_hbm, bins), (resp_hbm, resp),
            ]
        )
    ]
    for copy in copies:
        copy.start()
    tiles = acc.shape[0] - 1
    chunks = resp.shape[1] // CHUNK
    per_chunk = CHUNK // LANES
    zero_tile = jnp.zeros(acc.shape[1:], F32)

    def clear(t, carry):
        acc[t] = zero_tile
        return carry

    lax.fori_loop(0, tiles + 1, clear, 0)
    for copy in copies:
        copy.wait()
    nominal_rows[...] = nominal[...].astype(F32)
    knob_throws = throws[...].astype(F32).T.astype(jnp.bfloat16)
    bin_iota = lax.broadcasted_iota(jnp.int32, (2 * LANES, CHUNK), 0)

    def row_of(ref, i):
        return jnp.concatenate(
            [ref[pl.ds(i * per_chunk + g, 1), :] for g in range(per_chunk)], axis=1
        )

    def first_tile(i):
        return edges[i * per_chunk, 0] // LANES

    def weigh(i, slot):
        at = pl.ds(pl.multiple_of(i * CHUNK, CHUNK), CHUNK)
        nominal_row = row_of(nominal_rows, i)
        log_weight = jnp.dot(knob_throws, resp[:, at], preferred_element_type=F32)
        weights[slot, : 4 * QUARTER] = (nominal_row * jnp.exp(log_weight)).astype(jnp.bfloat16)
        weights[slot, 4 * QUARTER :] = jnp.broadcast_to(nominal_row, (16, CHUNK)).astype(
            jnp.bfloat16
        )

    def add_window(i, slot, tile):
        local = row_of(bins, i) - tile * LANES
        onehot = jnp.where(bin_iota == local, 1.0, 0.0).astype(jnp.bfloat16)
        part = lax.dot_general(
            weights[slot], onehot, (((1,), (1,)), ((), ())), preferred_element_type=F32
        )
        low, high = acc[tile] + part[:, :LANES], acc[tile + 1] + part[:, LANES:]
        acc[tile] = low
        acc[tile + 1] = high

    def add_rest(i, slot):
        first = first_tile(i)
        last = edges[i * per_chunk + per_chunk - 1, LANES - 1] // LANES

        def more(w, c):
            add_window(i, slot, first + 2 * w)
            return c

        lax.fori_loop(1, (last - first) // 2 + 1, more, 0)

    weigh(0, 0)

    def step(j, carry):
        weigh(2 * j + 1, 1)
        add_window(2 * j, 0, first_tile(2 * j))
        add_rest(2 * j, 0)
        weigh(jnp.minimum(2 * j + 2, chunks - 1), 0)
        add_window(2 * j + 1, 1, first_tile(2 * j + 1))
        add_rest(2 * j + 1, 1)
        return carry

    lax.fori_loop(0, chunks // 2, step, 0)

    def arrange(zb, carry):
        for half in range(2):
            tile = acc[2 * zb + half]
            for quarter in range(4):
                dest = out.at[quarter % 2, zb, quarter // 2]
                dest[half * QUARTER : (half + 1) * QUARTER] = tile[
                    quarter * QUARTER : (quarter + 1) * QUARTER
                ]
        low = acc[2 * zb, 4 * QUARTER : 4 * QUARTER + 8]
        high = acc[2 * zb + 1, 4 * QUARTER : 4 * QUARTER + 8]
        row = lax.broadcasted_iota(jnp.int32, (8, LANES), 0)
        both = jnp.where(row == 0, low, high)
        for quarter in range(4):
            out[quarter % 2, zb, quarter // 2, 2 * QUARTER :] = both
        return carry

    lax.fori_loop(0, tiles // 2, arrange, 0)


def histogram(responses, event_bins, nominal_weight, throws, bins_total):
    events = event_bins.shape[0]
    tiles = bins_total // LANES
    bins = event_bins.reshape(events // LANES, LANES)
    vmem = pl.BlockSpec(memory_space=pltpu.VMEM)
    return pl.pallas_call(
        hist_kernel,
        out_shape=jax.ShapeDtypeStruct((2, tiles // 2, 2, BLOCK_ROWS, LANES), F32),
        in_specs=[pl.BlockSpec(memory_space=pltpu.HBM)] * 4,
        out_specs=vmem,
        scratch_shapes=[
            pltpu.VMEM((tiles + 1, 4 * QUARTER + 16, LANES), F32),
            pltpu.VMEM((2, 4 * QUARTER + 16, CHUNK), jnp.bfloat16),
            pltpu.VMEM((events // LANES, LANES), F32),
            pltpu.VMEM(responses.shape, responses.dtype),
            pltpu.VMEM((events // LANES, LANES), jnp.int32),
            pltpu.VMEM((events // LANES, LANES), nominal_weight.dtype),
            pltpu.VMEM(throws.shape, throws.dtype),
            pltpu.SMEM((events // LANES, LANES), jnp.int32),
            pltpu.SemaphoreType.DMA((5,)),
        ],
        compiler_params=pltpu.CompilerParams(vmem_limit_bytes=VMEM_GRANT),
        name="histogram",
    )(*[pltpu.with_memory_space_constraint(x, pltpu.HBM) for x in (responses, bins, nominal_weight.reshape(events // LANES, LANES), throws)])


def exchange_kernel(
    nz, nu, spec_scale, cov_scale,
    part, spectra, cov,
    core_in, summed, x_in, ring_out, ring_in, own, dev, blocks,
    rows_in, cols_in, spec_in, prod, prod_in, pack_out, pack_in,
    core_s, core_r, x_s, x_r, ring_s, ring_r,
    blk_s, blk_r, fwd_s, rows_r, cols_s, cols_r, spec_s, spec_r, tail_s, tail_r,
):
    ev = lax.axis_index("ev")
    u = lax.axis_index("uni")
    z = ev // 4
    xl = lax.rem(ev // 2, 2)
    c = lax.rem(ev, 2)
    core_ev = ev + 1 - 2 * c
    x_ev = ev + 2 - 4 * xl
    diag_ev = x_ev + 1 - 2 * c
    half = nz // 2
    sum_skip = half // 2
    blk_skip = half // 2 + 1
    slots = nz // nu

    def along(d):
        return lax.rem(ev + 4 * (d % nz), 4 * nz)

    def z_at(d):
        return lax.rem(z + d % nz, nz)

    def send(src, dst, ssem, rsem, to_ev=ev, to_u=u):
        return pltpu.make_async_remote_copy(
            src_ref=src, dst_ref=dst, send_sem=ssem, recv_sem=rsem,
            device_id={"ev": to_ev, "uni": to_u}, device_id_type=MESH,
        )

    def block_of(k):
        j = (k + 1) // 2
        away = jnp.where(lax.rem(k, 2) == 1, half - j, nz - half + j)
        return lax.rem(z + away, nz)

    barrier = pltpu.get_barrier_semaphore()
    peers = [core_ev, x_ev, diag_ev]
    for d in sorted({1, sum_skip, blk_skip}):
        peers += [along(d), along(-d)]
    for peer in peers:
        pl.semaphore_signal(barrier, inc=1, device_id={"ev": peer, "uni": u}, device_id_type=MESH)
    for j in range(1, nu):
        pl.semaphore_signal(
            barrier, inc=1, device_id={"ev": ev, "uni": lax.rem(u + j, nu)}, device_id_type=MESH
        )
    pl.semaphore_wait(barrier, len(peers) + nu - 1)

    def core_copy(k):
        zb = block_of(k)
        return send(part.at[1 - c, zb], core_in.at[zb], core_s.at[k], core_r.at[k], to_ev=core_ev)

    def x_copy(k):
        zb = block_of(k)
        return send(summed.at[zb, 1 - xl], x_in.at[zb], x_s.at[k], x_r.at[k], to_ev=x_ev)

    def start_core(k, carry):
        core_copy(k).start()
        return carry

    lax.fori_loop(0, nz, start_core, 0)

    def start_x(k, carry):
        zb = block_of(k)
        core_copy(k).wait_recv()
        summed[zb] = part[c, zb] + core_in[zb]
        x_copy(k).start()
        return carry

    lax.fori_loop(0, nz, start_x, 0)

    sends = []
    arrivals = {}

    def ring_copy(n, way, to):
        return send(ring_out.at[n], ring_in.at[n], ring_s.at[n], ring_r.at[n], to_ev=along(way * to))

    def sum_step(way, d, first, to):
        n = len(sends)
        k = 0 if d == half else 2 * (half - d) - (way > 0)
        x_copy(k).wait_recv()
        zb = z_at(way * d)
        value = summed[zb, xl] + x_in[zb]
        if not first:
            slot, before = arrivals[way, d + 1]
            before.wait_recv()
            value = value + ring_in[slot]
        ring_out[n] = value
        copy = ring_copy(n, way, to)
        copy.start()
        sends.append(copy)
        arrivals[way, d] = n, copy

    order = []
    for d in range(half, sum_skip - 1, -1):
        for way in (1, -1):
            if way * d > -half:
                first = d == half or (way < 0 and d == half - 1)
                order.append((way, d, first, sum_skip if d == sum_skip else 1))
    near = [(way, d, d == sum_skip - 1, 1) for d in range(sum_skip - 1, 0, -1) for way in (1, -1)]
    order = order[:-2] + near[:2] + order[-2:] + near[2:]
    for step in order:
        sum_step(*step)
    x_copy(nz - 1).wait_recv()
    total = summed[z, xl] + x_in[z]
    finals = [arrivals[way, sum_skip] for way in (1, -1)]
    if sum_skip > 1:
        finals += [arrivals[way, 1] for way in (1, -1)]
    for slot, copy in finals:
        copy.wait_recv()
        total = total + ring_in[slot]
    own[...] = total
    dev[:QUARTER] = total[:QUARTER] - total[2 * QUARTER : 2 * QUARTER + 1]
    dev[QUARTER:] = total[QUARTER : 2 * QUARTER] - total[2 * QUARTER + 1 : 2 * QUARTER + 2]

    slot_of = {}
    blk_sends = []

    def block_copy(src, way, d, to):
        n = slot_of.setdefault((way, d), len(slot_of))
        copy = send(src, blocks.at[n], blk_s.at[n], blk_r.at[n], to_ev=along(way * to))
        copy.start()
        blk_sends.append(copy)

    def forward(n, src, origin, waiting=False):
        owner = origin // slots
        slot = lax.rem(origin, slots)

        @pl.when(owner != u)
        def _():
            copy = send(src, rows_in.at[slot, u], fwd_s.at[n], rows_r.at[slot, u], to_u=owner)
            if waiting:
                copy.wait_send()
            else:
                copy.start()

        if not waiting:

            @pl.when(owner == u)
            def _():
                rows_in[slot, u] = src[...]

    reach = {1: half, -1: half - 1}
    for way in (1, -1):
        if blk_skip <= reach[way]:
            block_copy(dev, way, blk_skip, blk_skip)
    for way in (1, -1):
        block_copy(dev, way, 1, 1)

    def cols_copy(j):
        return send(dev, cols_in.at[u], cols_s.at[j], cols_r.at[u], to_u=lax.rem(u + j, nu))

    def start_cols(j, carry):
        cols_copy(j).start()
        return carry

    lax.fori_loop(1, nu, start_cols, 0)
    forward(0, dev, z)
    cols_in[u] = dev[...]

    mine = 2 * xl + c
    spec_peers = ((core_ev, xl), (x_ev, 1 - xl), (diag_ev, 1 - xl))

    def spec_copy(i):
        peer, peer_half = spec_peers[i]
        src = own.at[pl.ds(pl.multiple_of(peer_half * QUARTER, QUARTER), QUARTER)]
        return send(src, spec_in.at[mine], spec_s.at[i], spec_r.at[i], to_ev=peer)

    for i in range(3):
        spec_copy(i).start()
    spec_in[mine] = own[pl.ds(pl.multiple_of(xl * QUARTER, QUARTER), QUARTER)]

    forwards = []

    def block_step(way, d):
        n = slot_of[way, d]
        send(dev, blocks.at[n], blk_s.at[n], blk_r.at[n], to_ev=along(way)).wait_recv()
        if d + 1 <= reach[way] and d + 1 != blk_skip:
            block_copy(blocks.at[n], way, d + 1, 1)
        forwards.append((blocks.at[n], z_at(-way * d)))
        forward(len(forwards), *forwards[-1])

    near = list(range(1, blk_skip))
    far = list(range(blk_skip, half + 1))
    order = near[:2]
    for i in range(max(len(far), len(near) - 2)):
        order += far[i : i + 1] + near[i + 2 : i + 3]
    for d in order:
        for way in (1, -1):
            if d <= reach[way]:
                block_step(way, d)

    for i in range(3):
        spec_copy(i).wait_recv()
    by_bin = spec_in[...].reshape(4 * QUARTER, LANES).T
    spectra[...] = jnp.where(c == 0, by_bin[: LANES // 2], by_bin[LANES // 2 :]) * spec_scale

    def wait_cols(j, carry):
        v = lax.rem(u + j, nu)
        send(dev, cols_in.at[v], cols_s.at[j], cols_r.at[v], to_u=v).wait_recv()
        return carry

    lax.fori_loop(1, nu, wait_cols, 0)

    depth = nu * QUARTER
    bf16 = jnp.bfloat16
    lane = lax.broadcasted_iota(jnp.int32, (depth, LANES), 1)
    left = cols_in[:, :QUARTER].reshape(depth, LANES)
    right = cols_in[:, QUARTER:].reshape(depth, LANES)
    cols = jnp.concatenate(
        [
            jnp.where(lane < LANES // 2, left, pltpu.roll(right, LANES // 2, 1)).T,
            jnp.where(lane < LANES // 2, pltpu.roll(left, LANES // 2, 1), right).T,
        ],
        axis=0,
    )
    cols_hi = cols.astype(bf16)
    cols_lo = (cols - cols_hi.astype(F32)).astype(bf16)
    cols_all = jnp.concatenate([cols_hi, cols_hi, cols_lo], axis=1)
    xl_rows = pl.ds(pl.multiple_of((1 - xl) * (LANES // 2), LANES // 2), LANES // 2)
    my_rows = pl.ds(pl.multiple_of(xl * (LANES // 2), LANES // 2), LANES // 2)

    def core_tail(slot):
        return send(
            prod.at[slot, 1 - c], prod_in.at[slot], tail_s.at[0, slot], tail_r.at[0, slot],
            to_ev=core_ev,
        )

    def x_tail(slot):
        return send(
            pack_out.at[slot], pack_in.at[slot], tail_s.at[1, slot], tail_r.at[1, slot], to_ev=x_ev
        )

    for slot in range(slots):

        def wait_rows(j, carry, slot=slot):
            v = lax.rem(u + j, nu)
            send(dev, rows_in.at[slot, v], cols_s.at[0], rows_r.at[slot, v], to_u=v).wait_recv()
            return carry

        lax.fori_loop(1, nu, wait_rows, 0)
        rows = jnp.concatenate(
            [
                rows_in[slot, :, :QUARTER].reshape(depth, LANES),
                rows_in[slot, :, QUARTER:].reshape(depth, LANES),
            ],
            axis=1,
        )
        rows_hi = rows.astype(bf16)
        rows_lo = (rows - rows_hi.astype(F32)).astype(bf16)
        rows_all = jnp.concatenate([rows_hi, rows_lo, rows_hi], axis=0)
        product = jnp.dot(cols_all, rows_all, preferred_element_type=F32)
        prod[slot, 0] = product[:LANES]
        prod[slot, 1] = product[LANES:]
        core_tail(slot).start()
    for slot in range(slots):
        core_tail(slot).wait_recv()
        pack_out[slot] = prod[slot, c, xl_rows] + prod_in[slot, xl_rows]
        x_tail(slot).start()
    for slot in range(slots):
        x_tail(slot).wait_recv()
        keep = prod[slot, c, my_rows] + prod_in[slot, my_rows]
        cov[:, slot * 2 * LANES : (slot + 1) * 2 * LANES] = (keep + pack_in[slot]) * cov_scale

    def drain(k, carry):
        core_copy(k).wait_send()
        x_copy(k).wait_send()
        return carry

    lax.fori_loop(0, nz, drain, 0)
    for copy in sends + blk_sends:
        copy.wait_send()
    forward(0, dev, z, waiting=True)
    for n, (src, origin) in enumerate(forwards):
        forward(n + 1, src, origin, waiting=True)

    def drain_cols(j, carry):
        cols_copy(j).wait_send()
        return carry

    lax.fori_loop(1, nu, drain_cols, 0)
    for i in range(3):
        spec_copy(i).wait_send()
    for slot in range(slots):
        core_tail(slot).wait_send()
        x_tail(slot).wait_send()


def exchange(part, nz, nu, spec_scale, cov_scale):
    slots = nz // nu
    rows = slots * 2 * LANES
    block = (BLOCK_ROWS, LANES)
    blk = (2 * QUARTER, LANES)
    vmem = pl.BlockSpec(memory_space=pltpu.VMEM)

    def buf(*shape):
        return pltpu.VMEM(shape, F32)

    def dma(*shape):
        return pltpu.SemaphoreType.DMA(shape)

    spectra, cov = pl.pallas_call(
        functools.partial(exchange_kernel, nz, nu, spec_scale, cov_scale),
        out_shape=(
            jax.ShapeDtypeStruct((LANES // 2, 4 * QUARTER), F32),
            jax.ShapeDtypeStruct((LANES // 2, rows), F32),
        ),
        in_specs=[vmem],
        out_specs=(vmem, vmem),
        scratch_shapes=[
            buf(nz, 2, *block),
            buf(nz, 2, *block),
            buf(nz, *block),
            buf(nz - 1, *block), buf(nz - 1, *block),
            buf(*block), buf(*blk),
            buf(nz - 1, *blk),
            buf(slots, nu, *blk), buf(nu, *blk),
            buf(4, QUARTER, LANES),
            buf(slots, 2, LANES, 2 * LANES), buf(slots, LANES, 2 * LANES),
            buf(slots, LANES // 2, 2 * LANES), buf(slots, LANES // 2, 2 * LANES),
            dma(nz), dma(nz), dma(nz), dma(nz),
            dma(nz - 1), dma(nz - 1),
            dma(nz - 1), dma(nz - 1),
            dma(nz), dma(slots, nu), dma(nu), dma(nu),
            dma(3), dma(3), dma(2, slots), dma(2, slots),
        ],
        compiler_params=pltpu.CompilerParams(
            collective_id=0, has_side_effects=True, vmem_limit_bytes=VMEM_GRANT
        ),
        name="exchange",
    )(part)
    return spectra, cov.T


def body(responses, event_bins, nominal_weight, throws):
    nz = lax.axis_size("ev") // 4
    nu = lax.axis_size("uni")
    bins_total = nz * 2 * LANES
    per_bin = event_bins.shape[0] * lax.axis_size("ev") // bins_total
    universes = throws.shape[1] * nu
    part = histogram(responses, event_bins, nominal_weight, throws, bins_total)
    return exchange(part, nz, nu, 1.0 / per_bin, 1.0 / (universes * per_bin))


def solution(mesh):
    in_specs = (P(None, "ev"), P("ev"), P("ev"), P(None, "uni"))
    out_specs = (P("ev", "uni"), P("uni", "ev"))
    return jax.shard_map(body, mesh=mesh, in_specs=in_specs, out_specs=out_specs, check_vma=False)
```

time: 106 us -> 85 us (0.80)
  Pallas kernels: 97 us -> 82.9 us
  local copies, waits for them, and re-layouts: 4.74 us -> 1.27 us
  other arithmetic: 2.83 us -> 0 us
    pallas_call x1, Pallas kernels: 82.4 us -> 71.7 us  [exchange(): pl.pallas_call(functools.partial(exchange_kernel, nz, nu, spec_scale, cov...]
    pallas_call x1, Pallas kernels: 14.7 us -> 11.2 us  [histogram(): pl.pallas_call(hist_kernel, out_shape=jax.ShapeDtypeStruct((2, tiles // 2...]
    pallas_call x1 -> x0, local copies, waits for them, and re-layouts: 1.72 us -> none  [exchange(): pl.pallas_call(functools.partial(exchange_kernel, nz, nu, spec_scale, cov...]
    reshape x1 -> x0, other arithmetic: 1.39 us -> none  [histogram(): nominal_weight.astype(F32).reshape(1, events)]
where the time goes in v2:
time: 85 us; the launch traced here: 84.8 us
  Pallas kernels  82.9 us (98%)
  local copies, waits for them, and re-layouts  1.27 us (1%)
    pallas_call x1, Pallas kernels, exchange(): pl.pallas_call(functools.partial(exchange_kernel, nz, nu, spec_scale, cov...  71.7 us
    pallas_call x1, Pallas kernels, histogram(): pl.pallas_call(hist_kernel, out_shape=jax.ShapeDtypeStruct((2, tiles // 2...  11.2 us

profile of v2, /device:TPU:5, one launch (start us, length us, event | category | flops | bytes accessed | tf_op | source)
XLA Modules:
  0.0 84.8 jit_solution(4050909468147710532)
XLA Ops:
  0.6 11.2 %histogram.1.part = f32[2,16,2,72,128]{4,3,2,1,0:T(8,128)S(1)} custom-call(bf16[64,16384]{1,0:T(8,128)(2,1)} %resp_hbm.1, s32[128,128]{1,0:T(8,128)} %bitcast.4, bf16[128,128]{1,0:T(8,128)(2,1)} %bitcast.5, s32[64,128]{1,0:T(8,128)} %throws_hbm.1), custom_call_target="tpu_custom_call" | custom-call | tf_op jit(solution)/shard_map/histogram/pallas_call | solution.py:125
  11.8 71.7 %exchange.1 = (f32[64,128]{1,0:T(8,128)S(1)}, f32[64,512]{1,0:T(8,128)S(1)}) custom-call(f32[2,16,2,72,128]{4,3,2,1,0:T(8,128)S(1)} %histogram.1.part), custom_call_target="tpu_custom_call" | custom-call | tf_op jit(solution)/shard_map/exchange/pallas_call | solution.py:449
  83.5 0.6 copy.8
  84.2 0.7 copy.9

commit v3 on v2

--- a/solution.py
+++ b/solution.py
@@ -11,141 +11,194 @@
 QUARTER = 32
 BLOCK_ROWS = 72
 CHUNK = 512
+WINDOW = 1280
+LAG = 7
 VMEM_GRANT = 20 << 20
 MESH = pl.DeviceIdType.MESH
 F32 = jnp.float32
 
 
-def hist_kernel(
+def block_histogram(weights, local):
+    iota = lax.broadcasted_iota(jnp.int32, (2 * LANES, local.shape[1]), 0)
+    onehot = jnp.where(iota == local, 1.0, 0.0).astype(jnp.bfloat16)
+    return lax.dot_general(
+        weights, onehot, (((1,), (1,)), ((), ())), preferred_element_type=F32
+    )
+
+
+def weigh(knob_throws, resp, nominal_row):
+    log_weight = jnp.dot(knob_throws, resp, preferred_element_type=F32)
+    return (nominal_row * jnp.exp(log_weight)).astype(jnp.bfloat16)
+
+
+def central_rows(nominal_row):
+    return jnp.broadcast_to(nominal_row, (16, nominal_row.shape[1])).astype(jnp.bfloat16)
+
+
+def rows_of(ref, start, count):
+    return jnp.concatenate([ref[pl.ds(start + g, 1), :] for g in range(count)], axis=1)
+
+
+def quarter_blocks(sums):
+    row = lax.broadcasted_iota(jnp.int32, (8, LANES), 0)
+    tail = sums[4 * QUARTER : 4 * QUARTER + 8]
+    central = jnp.where(row == 0, tail[:, :LANES], tail[:, LANES:])
+    for quarter in range(4):
+        mine = sums[quarter * QUARTER : (quarter + 1) * QUARTER]
+        block = jnp.concatenate([mine[:, :LANES], mine[:, LANES:], central], axis=0)
+        yield quarter % 2, quarter // 2, block
+
+
+def windows_kernel(
     resp_hbm, bins_hbm, nominal_hbm, throws_hbm,
-    out,
-    acc, weights, nominal_rows, resp, bins, nominal, throws, edges, sems,
+    resp_of, local_of, nominal_of, throws_t, extra,
+    resp, bins, nominal, throws, nominal_rows, acc, starts, sems, resp_sems,
 ):
-    copies = [
+    nz = resp_of.shape[0]
+    per_row = LANES
+    rows = bins_hbm.shape[0]
+    window = WINDOW // LANES
+    loads = [
         pltpu.make_async_copy(src, dst, sems.at[i])
         for i, (src, dst) in enumerate(
-            [
-                (throws_hbm, throws), (bins_hbm, edges), (nominal_hbm, nominal),
-                (bins_hbm, bins), (resp_hbm, resp),
-            ]
+            [(bins_hbm, bins), (nominal_hbm, nominal), (throws_hbm, throws)]
         )
     ]
-    for copy in copies:
-        copy.start()
-    tiles = acc.shape[0] - 1
-    chunks = resp.shape[1] // CHUNK
-    per_chunk = CHUNK // LANES
-    zero_tile = jnp.zeros(acc.shape[1:], F32)
-
-    def clear(t, carry):
-        acc[t] = zero_tile
-        return carry
-
-    lax.fori_loop(0, tiles + 1, clear, 0)
-    for copy in copies:
-        copy.wait()
+    for load in loads:
+        load.start()
+
+    def clear(zb, carry):
+        extra[:, zb] = jnp.zeros((2, 2, BLOCK_ROWS, LANES), F32)
+        return carry
+
+    lax.fori_loop(0, nz, clear, 0)
+    for load in loads:
+        load.wait()
+    all_bins = bins[...]
+    below = [jnp.int32(0)]
+    for zb in range(1, nz):
+        hits = jnp.sum(jnp.where(all_bins < zb * 2 * LANES, 1.0, 0.0), axis=0, keepdims=True)
+        below.append(jnp.sum(hits).astype(jnp.int32))
+    below.append(jnp.int32(rows * LANES))
+    beyond = jnp.int32(0)
+    for zb in range(nz):
+        start = jnp.minimum(below[zb] // LANES, rows - window)
+        starts[zb] = start
+        beyond = jnp.maximum(beyond, below[zb + 1] - (start + window) * LANES)
+
+    def resp_copy(zb):
+        events = pl.ds(pl.multiple_of(starts[zb] * LANES, LANES), WINDOW)
+        return pltpu.make_async_copy(resp_hbm.at[:, events], resp_of.at[zb], resp_sems.at[zb])
+
+    def start_copy(zb, carry):
+        resp_copy(zb).start()
+        return carry
+
+    lax.fori_loop(0, nz, start_copy, 0)
     nominal_rows[...] = nominal[...].astype(F32)
     knob_throws = throws[...].astype(F32).T.astype(jnp.bfloat16)
-    bin_iota = lax.broadcasted_iota(jnp.int32, (2 * LANES, CHUNK), 0)
-
-    def row_of(ref, i):
-        return jnp.concatenate(
-            [ref[pl.ds(i * per_chunk + g, 1), :] for g in range(per_chunk)], axis=1
-        )
-
-    def first_tile(i):
-        return edges[i * per_chunk, 0] // LANES
-
-    def weigh(i, slot):
-        at = pl.ds(pl.multiple_of(i * CHUNK, CHUNK), CHUNK)
-        nominal_row = row_of(nominal_rows, i)
-        log_weight = jnp.dot(knob_throws, resp[:, at], preferred_element_type=F32)
-        weights[slot, : 4 * QUARTER] = (nominal_row * jnp.exp(log_weight)).astype(jnp.bfloat16)
-        weights[slot, 4 * QUARTER :] = jnp.broadcast_to(nominal_row, (16, CHUNK)).astype(
-            jnp.bfloat16
-        )
-
-    def add_window(i, slot, tile):
-        local = row_of(bins, i) - tile * LANES
-        onehot = jnp.where(bin_iota == local, 1.0, 0.0).astype(jnp.bfloat16)
-        part = lax.dot_general(
-            weights[slot], onehot, (((1,), (1,)), ((), ())), preferred_element_type=F32
-        )
-        low, high = acc[tile] + part[:, :LANES], acc[tile + 1] + part[:, LANES:]
-        acc[tile] = low
-        acc[tile + 1] = high
-
-    def add_rest(i, slot):
-        first = first_tile(i)
-        last = edges[i * per_chunk + per_chunk - 1, LANES - 1] // LANES
-
-        def more(w, c):
-            add_window(i, slot, first + 2 * w)
-            return c
-
-        lax.fori_loop(1, (last - first) // 2 + 1, more, 0)
-
-    weigh(0, 0)
-
-    def step(j, carry):
-        weigh(2 * j + 1, 1)
-        add_window(2 * j, 0, first_tile(2 * j))
-        add_rest(2 * j, 0)
-        weigh(jnp.minimum(2 * j + 2, chunks - 1), 0)
-        add_window(2 * j + 1, 1, first_tile(2 * j + 1))
-        add_rest(2 * j + 1, 1)
-        return carry
-
-    lax.fori_loop(0, chunks // 2, step, 0)
-
-    def arrange(zb, carry):
-        for half in range(2):
-            tile = acc[2 * zb + half]
-            for quarter in range(4):
-                dest = out.at[quarter % 2, zb, quarter // 2]
-                dest[half * QUARTER : (half + 1) * QUARTER] = tile[
-                    quarter * QUARTER : (quarter + 1) * QUARTER
-                ]
-        low = acc[2 * zb, 4 * QUARTER : 4 * QUARTER + 8]
-        high = acc[2 * zb + 1, 4 * QUARTER : 4 * QUARTER + 8]
-        row = lax.broadcasted_iota(jnp.int32, (8, LANES), 0)
-        both = jnp.where(row == 0, low, high)
-        for quarter in range(4):
-            out[quarter % 2, zb, quarter // 2, 2 * QUARTER :] = both
-        return carry
-
-    lax.fori_loop(0, tiles // 2, arrange, 0)
-
-
-def histogram(responses, event_bins, nominal_weight, throws, bins_total):
-    events = event_bins.shape[0]
-    tiles = bins_total // LANES
-    bins = event_bins.reshape(events // LANES, LANES)
+    throws_t[...] = knob_throws
+
+    def take(zb, carry):
+        at = starts[zb]
+        for g in range(window):
+            lanes = slice(g * LANES, (g + 1) * LANES)
+            local_of[zb, :, lanes] = bins[pl.ds(at + g, 1), :] - zb * 2 * LANES
+            nominal_of[zb, :, lanes] = nominal_rows[pl.ds(at + g, 1), :]
+        return carry
+
+    lax.fori_loop(0, nz, take, 0)
+
+    @pl.when(beyond > 0)
+    def _():
+        copy = pltpu.make_async_copy(resp_hbm, resp, sems.at[3])
+        copy.start()
+        copy.wait()
+        count = CHUNK // LANES
+
+        def one_block(zb, carry):
+            acc[...] = jnp.zeros(acc.shape, F32)
+            first = starts[zb] + window
+
+            def one_chunk(row, c):
+                at = jnp.minimum(row, rows - count)
+                nominal_row = rows_of(nominal_rows, at, count)
+                events = pl.ds(pl.multiple_of(at * LANES, LANES), CHUNK)
+                index = at * LANES + lax.broadcasted_iota(jnp.int32, (1, CHUNK), 1)
+                bin_row = jnp.where(index >= row * LANES, rows_of(bins, at, count), -1)
+                all_weights = jnp.concatenate(
+                    [weigh(knob_throws, resp[:, events], nominal_row), central_rows(nominal_row)],
+                    axis=0,
+                )
+                acc[...] += block_histogram(all_weights, bin_row - zb * 2 * LANES)
+                return c
+
+            def step(i, c):
+                row = first + i * count
+
+                @pl.when(row < rows)
+                def _():
+                    @pl.when(bins_row_min(bins, row) < (zb + 1) * 2 * LANES)
+                    def _():
+                        one_chunk(row, 0)
+
+                return c
+
+            lax.fori_loop(0, rows // count, step, 0)
+            for c, x, block in quarter_blocks(acc[...]):
+                extra[c, zb, x] = block
+            return carry
+
+        lax.fori_loop(0, nz, one_block, 0)
+
+    def wait_copy(zb, carry):
+        resp_copy(zb).wait()
+        return carry
+
+    lax.fori_loop(0, nz, wait_copy, 0)
+
+
+def bins_row_min(bins, row):
+    return jnp.min(bins[pl.ds(row, 1), :])
+
+
+def windows(responses, bins, nominal, throws, nz):
+    rows = bins.shape[0]
+    hbm = pl.BlockSpec(memory_space=pltpu.HBM)
     vmem = pl.BlockSpec(memory_space=pltpu.VMEM)
+    shape = jax.ShapeDtypeStruct
     return pl.pallas_call(
-        hist_kernel,
-        out_shape=jax.ShapeDtypeStruct((2, tiles // 2, 2, BLOCK_ROWS, LANES), F32),
-        in_specs=[pl.BlockSpec(memory_space=pltpu.HBM)] * 4,
-        out_specs=vmem,
+        windows_kernel,
+        out_shape=(
+            shape((nz, responses.shape[0], WINDOW), responses.dtype),
+            shape((nz, 1, WINDOW), jnp.int32),
+            shape((nz, 1, WINDOW), F32),
+            shape(throws.shape[::-1], jnp.bfloat16),
+            shape((2, nz, 2, BLOCK_ROWS, LANES), F32),
+        ),
+        in_specs=[hbm] * 4,
+        out_specs=(vmem,) * 5,
         scratch_shapes=[
-            pltpu.VMEM((tiles + 1, 4 * QUARTER + 16, LANES), F32),
-            pltpu.VMEM((2, 4 * QUARTER + 16, CHUNK), jnp.bfloat16),
-            pltpu.VMEM((events // LANES, LANES), F32),
             pltpu.VMEM(responses.shape, responses.dtype),
-            pltpu.VMEM((events // LANES, LANES), jnp.int32),
-            pltpu.VMEM((events // LANES, LANES), nominal_weight.dtype),
+            pltpu.VMEM(bins.shape, jnp.int32),
+            pltpu.VMEM(nominal.shape, nominal.dtype),
             pltpu.VMEM(throws.shape, throws.dtype),
-            pltpu.SMEM((events // LANES, LANES), jnp.int32),
-            pltpu.SemaphoreType.DMA((5,)),
+            pltpu.VMEM((rows, LANES), F32),
+            pltpu.VMEM((4 * QUARTER + 16, 2 * LANES), F32),
+            pltpu.SMEM((nz,), jnp.int32),
+            pltpu.SemaphoreType.DMA((4,)),
+            pltpu.SemaphoreType.DMA((nz,)),
         ],
         compiler_params=pltpu.CompilerParams(vmem_limit_bytes=VMEM_GRANT),
-        name="histogram",
-    )(*[pltpu.with_memory_space_constraint(x, pltpu.HBM) for x in (responses, bins, nominal_weight.reshape(events // LANES, LANES), throws)])
+        name="windows",
+    )(responses, bins, nominal, throws)
 
 
 def exchange_kernel(
     nz, nu, spec_scale, cov_scale,
-    part, spectra, cov,
+    resp_of, local_of, nominal_of, throws_t, extra,
+    spectra, cov,
+    part,
     core_in, summed, x_in, ring_out, ring_in, own, dev, blocks,
     rows_in, cols_in, spec_in, prod, prod_in, pack_out, pack_in,
     core_s, core_r, x_s, x_r, ring_s, ring_r,
@@ -191,6 +244,7 @@
         pl.semaphore_signal(
             barrier, inc=1, device_id={"ev": ev, "uni": lax.rem(u + j, nu)}, device_id_type=MESH
         )
+    knob_throws = throws_t[...]
     pl.semaphore_wait(barrier, len(peers) + nu - 1)
 
     def core_copy(k):
@@ -201,61 +255,69 @@
         zb = block_of(k)
         return send(summed.at[zb, 1 - xl], x_in.at[zb], x_s.at[k], x_r.at[k], to_ev=x_ev)
 
-    def start_core(k, carry):
+    def histogram(k):
+        zb = block_of(k)
+        nominal_row = nominal_of[zb]
+        weights = jnp.concatenate(
+            [weigh(knob_throws, resp_of[zb], nominal_row), central_rows(nominal_row)], axis=0
+        )
+        sums = block_histogram(weights, local_of[zb])
+        for to_core, to_x, block in quarter_blocks(sums):
+            part[to_core, zb, to_x] = block + extra[to_core, zb, to_x]
         core_copy(k).start()
-        return carry
-
-    lax.fori_loop(0, nz, start_core, 0)
-
-    def start_x(k, carry):
+
+    def start_x(k):
         zb = block_of(k)
         core_copy(k).wait_recv()
         summed[zb] = part[c, zb] + core_in[zb]
         x_copy(k).start()
-        return carry
-
-    lax.fori_loop(0, nz, start_x, 0)
-
-    sends = []
-    arrivals = {}
-
-    def ring_copy(n, way, to):
-        return send(ring_out.at[n], ring_in.at[n], ring_s.at[n], ring_r.at[n], to_ev=along(way * to))
-
-    def sum_step(way, d, first, to):
-        n = len(sends)
-        k = 0 if d == half else 2 * (half - d) - (way > 0)
+
+    def ring_copy(k):
+        way = jnp.where((lax.rem(k, 2) == 1) | (k == 0), 1, -1)
+        to = jnp.where(half - (k + 1) // 2 == sum_skip, sum_skip, 1)
+        to_ev = lax.rem(ev + 4 * (nz + way * to), 4 * nz)
+        return send(ring_out.at[k], ring_in.at[k], ring_s.at[k], ring_r.at[k], to_ev=to_ev)
+
+    def sum_step(k):
+        zb = block_of(k)
         x_copy(k).wait_recv()
-        zb = z_at(way * d)
         value = summed[zb, xl] + x_in[zb]
-        if not first:
-            slot, before = arrivals[way, d + 1]
-            before.wait_recv()
-            value = value + ring_in[slot]
-        ring_out[n] = value
-        copy = ring_copy(n, way, to)
-        copy.start()
-        sends.append(copy)
-        arrivals[way, d] = n, copy
-
-    order = []
-    for d in range(half, sum_skip - 1, -1):
-        for way in (1, -1):
-            if way * d > -half:
-                first = d == half or (way < 0 and d == half - 1)
-                order.append((way, d, first, sum_skip if d == sum_skip else 1))
-    near = [(way, d, d == sum_skip - 1, 1) for d in range(sum_skip - 1, 0, -1) for way in (1, -1)]
-    order = order[:-2] + near[:2] + order[-2:] + near[2:]
-    for step in order:
-        sum_step(*step)
+        starts_chain = (k == 0) | (k == 2) | (half - (k + 1) // 2 == sum_skip - 1)
+
+        @pl.when(starts_chain)
+        def _():
+            ring_out[k] = value
+
+        @pl.when(jnp.logical_not(starts_chain))
+        def _():
+            before = jnp.maximum(k - 2, 0)
+            ring_copy(before).wait_recv()
+            ring_out[k] = value + ring_in[before]
+
+        ring_copy(k).start()
+
+    def block_step_of(k, carry):
+        @pl.when(k < nz)
+        def _():
+            histogram(k)
+
+        @pl.when((k > 0) & (k <= nz))
+        def _():
+            start_x(k - 1)
+
+        @pl.when(k >= LAG)
+        def _():
+            sum_step(k - LAG)
+
+        return carry
+
+    lax.fori_loop(0, nz - 1 + LAG, block_step_of, 0)
     x_copy(nz - 1).wait_recv()
     total = summed[z, xl] + x_in[z]
-    finals = [arrivals[way, sum_skip] for way in (1, -1)]
-    if sum_skip > 1:
-        finals += [arrivals[way, 1] for way in (1, -1)]
-    for slot, copy in finals:
-        copy.wait_recv()
-        total = total + ring_in[slot]
+    last_far = 2 * (half - sum_skip)
+    for k in sorted({last_far - 1, last_far, nz - 3, nz - 2}):
+        ring_copy(k).wait_recv()
+        total = total + ring_in[k]
     own[...] = total
     dev[:QUARTER] = total[:QUARTER] - total[2 * QUARTER : 2 * QUARTER + 1]
     dev[QUARTER:] = total[QUARTER : 2 * QUARTER] - total[2 * QUARTER + 1 : 2 * QUARTER + 2]
@@ -329,9 +391,9 @@
 
     near = list(range(1, blk_skip))
     far = list(range(blk_skip, half + 1))
-    order = near[:2]
-    for i in range(max(len(far), len(near) - 2)):
-        order += far[i : i + 1] + near[i + 2 : i + 3]
+    order = near[:1]
+    for i in range(max(len(far), len(near) - 1)):
+        order += far[i : i + 1] + near[i + 1 : i + 2]
     for d in order:
         for way in (1, -1):
             if d <= reach[way]:
@@ -415,7 +477,13 @@
         return carry
 
     lax.fori_loop(0, nz, drain, 0)
-    for copy in sends + blk_sends:
+
+    def drain_sums(k, carry):
+        ring_copy(k).wait_send()
+        return carry
+
+    lax.fori_loop(0, nz - 1, drain_sums, 0)
+    for copy in blk_sends:
         copy.wait_send()
     forward(0, dev, z, waiting=True)
     for n, (src, origin) in enumerate(forwards):
@@ -433,7 +501,7 @@
         x_tail(slot).wait_send()
 
 
-def exchange(part, nz, nu, spec_scale, cov_scale):
+def exchange(taken, nz, nu, spec_scale, cov_scale):
     slots = nz // nu
     rows = slots * 2 * LANES
     block = (BLOCK_ROWS, LANES)
@@ -452,9 +520,10 @@
             jax.ShapeDtypeStruct((LANES // 2, 4 * QUARTER), F32),
             jax.ShapeDtypeStruct((LANES // 2, rows), F32),
         ),
-        in_specs=[vmem],
+        in_specs=[vmem] * len(taken),
         out_specs=(vmem, vmem),
         scratch_shapes=[
+            buf(2, nz, 2, *block),
             buf(nz, 2, *block),
             buf(nz, 2, *block),
             buf(nz, *block),
@@ -475,7 +544,7 @@
             collective_id=0, has_side_effects=True, vmem_limit_bytes=VMEM_GRANT
         ),
         name="exchange",
-    )(part)
+    )(*taken)
     return spectra, cov.T
 
 
@@ -485,8 +554,15 @@
     bins_total = nz * 2 * LANES
     per_bin = event_bins.shape[0] * lax.axis_size("ev") // bins_total
     universes = throws.shape[1] * nu
-    part = histogram(responses, event_bins, nominal_weight, throws, bins_total)
-    return exchange(part, nz, nu, 1.0 / per_bin, 1.0 / (universes * per_bin))
+    rows = event_bins.shape[0] // LANES
+    inputs = [
+        pltpu.with_memory_space_constraint(x, pltpu.HBM)
+        for x in (
+            responses, event_bins.reshape(rows, LANES), nominal_weight.reshape(rows, LANES), throws
+        )
+    ]
+    taken = windows(*inputs, nz)
+    return exchange(taken, nz, nu, 1.0 / per_bin, 1.0 / (universes * per_bin))
 
 
 def solution(mesh):

time: 85 us -> 79.3 us (0.933)
  Pallas kernels: 82.9 us -> 77.2 us
    pallas_call x1, Pallas kernels: 11.2 us -> 3.12 us  [windows(): pl.pallas_call(windows_kernel, out_shape=(shape((nz, responses.shape[0],...]
    pallas_call x1, Pallas kernels: 71.7 us -> 74.1 us  [exchange(): pl.pallas_call(functools.partial(exchange_kernel, nz, nu, spec_scale, cov...]
where the time goes in v3:
time: 79.3 us; the launch traced here: 79.1 us
  Pallas kernels  77.2 us (97%)
  local copies, waits for them, and re-layouts  1.27 us (2%)
    pallas_call x1, Pallas kernels, exchange(): pl.pallas_call(functools.partial(exchange_kernel, nz, nu, spec_scale, cov...  74.1 us
    pallas_call x1, Pallas kernels, windows(): pl.pallas_call(windows_kernel, out_shape=(shape((nz, responses.shape[0],...  3.12 us

profile of v3, /device:TPU:5, one launch (start us, length us, event | category | flops | bytes accessed | tf_op | source)
XLA Modules:
  0.0 79.1 jit_solution(13897092010112822520)
XLA Ops:
  0.6 3.1 %windows.1 = (bf16[16,64,1280]{2,1,0:T(8,128)(2,1)S(1)}, s32[16,1,1280]{2,1,0:T(1,128)S(1)}, f32[16,1,1280]{2,1,0:T(1,128)S(1)}, bf16[128,64]{1,0:T(8,128)(2,1)S(1)}, f32[2,16,2,72,128]{4,3,2,1,0:T(8,128)S(1)}) custom-call(bf16[64,16384]{1,0:T(8,128)(2,1)} %resp_hbm.1, s32[128,128]{1,0:T(8,128)} %bitcast.4, bf16[128,128]{1,0:T(8,128)(2,1)} %bitcast.5, ...), custom_call_target="tpu_custom_call" | custom-call | tf_op jit(solution)/shard_map/windows/pallas_call | solution.py:170
  3.8 74.1 %exchange.1 = (f32[64,128]{1,0:T(8,128)S(1)}, f32[64,512]{1,0:T(8,128)S(1)}) custom-call(bf16[16,64,1280]{2,1,0:T(8,128)(2,1)S(1)} %get-tuple-element.9.resp_of, s32[16,1,1280]{2,1,0:T(1,128)S(1)} %get-tuple-element.10.local_of, f32[16,1,1280]{2,1,0:T(1,128)S(1)} %get-tuple-element.11.nominal_of, bf16[128,64]{1,0:T(8,128)(2,1)S(1)} %get-tuple-element.12.throws_t, ...), custom_call_target="tpu_custom_call" | custom-call | tf_op jit(solution)/shard_map/exchange/pallas_call | solution.py:517
  77.8 0.6 copy.8
  78.4 0.7 copy.9

commit v4 on v3

--- a/solution.py
+++ b/solution.py
@@ -12,7 +12,7 @@
 BLOCK_ROWS = 72
 CHUNK = 512
 WINDOW = 1280
-LAG = 7
+HOP = 3
 VMEM_GRANT = 20 << 20
 MESH = pl.DeviceIdType.MESH
 F32 = jnp.float32
@@ -213,9 +213,15 @@
     x_ev = ev + 2 - 4 * xl
     diag_ev = x_ev + 1 - 2 * c
     half = nz // 2
-    sum_skip = half // 2
-    blk_skip = half // 2 + 1
     slots = nz // nu
+    relays = half // HOP
+
+    def relay_of(d):
+        return min((d + 1) // HOP, relays)
+
+    targets = {r: [] for r in range(-relays, relays + 1)}
+    for d in range(1 - half, half + 1):
+        targets[relay_of(d)].append(d - HOP * relay_of(d))
 
     def along(d):
         return lax.rem(ev + 4 * (d % nz), 4 * nz)
@@ -234,18 +240,42 @@
         away = jnp.where(lax.rem(k, 2) == 1, half - j, nz - half + j)
         return lax.rem(z + away, nz)
 
+    def tell(to_ev, to_u=u):
+        pl.semaphore_signal(
+            barrier, inc=1, device_id={"ev": to_ev, "uni": to_u}, device_id_type=MESH
+        )
+
     barrier = pltpu.get_barrier_semaphore()
     peers = [core_ev, x_ev, diag_ev]
-    for d in sorted({1, sum_skip, blk_skip}):
+    for d in sorted({1} | {HOP * r for r in range(1, relays + 1)}):
         peers += [along(d), along(-d)]
     for peer in peers:
-        pl.semaphore_signal(barrier, inc=1, device_id={"ev": peer, "uni": u}, device_id_type=MESH)
+        tell(peer)
     for j in range(1, nu):
-        pl.semaphore_signal(
-            barrier, inc=1, device_id={"ev": ev, "uni": lax.rem(u + j, nu)}, device_id_type=MESH
-        )
+        tell(ev, lax.rem(u + j, nu))
+    expected = len(peers) + nu - 1
+    for slot in range(slots):
+        d = lax.rem(z - (u * slots + slot) + nz + half - 1, nz) - (half - 1)
+        relay = jnp.minimum((d + 1 + HOP * nz) // HOP - nz, relays)
+        away = d - HOP * relay
+        from_ev = lax.rem(ev + 4 * (nz - away), 4 * nz)
+
+        def tell_column(v, carry, from_ev=from_ev):
+            @pl.when((from_ev != ev) | (v != u))
+            def _():
+                tell(from_ev, v)
+
+            return carry
+
+        lax.fori_loop(0, nu, tell_column, 0)
+    for r, aways in targets.items():
+        for away in aways:
+            if away == 0:
+                expected = expected + jnp.where(z_at(-HOP * r) // slots == u, 0, 1)
+            else:
+                expected = expected + 1
     knob_throws = throws_t[...]
-    pl.semaphore_wait(barrier, len(peers) + nu - 1)
+    pl.semaphore_wait(barrier, expected)
 
     def core_copy(k):
         zb = block_of(k)
@@ -273,88 +303,90 @@
         x_copy(k).start()
 
     def ring_copy(k):
-        way = jnp.where((lax.rem(k, 2) == 1) | (k == 0), 1, -1)
-        to = jnp.where(half - (k + 1) // 2 == sum_skip, sum_skip, 1)
-        to_ev = lax.rem(ev + 4 * (nz + way * to), 4 * nz)
-        return send(ring_out.at[k], ring_in.at[k], ring_s.at[k], ring_r.at[k], to_ev=to_ev)
+        d, way = half - (k + 1) // 2, 1 if k % 2 or k == 0 else -1
+        to = d if d == 1 or d % HOP == 0 else 1
+        return send(
+            ring_out.at[k], ring_in.at[k], ring_s.at[k], ring_r.at[k], to_ev=along(way * to)
+        )
+
+    def starts_chain(k):
+        return k in (0, 2) or (half - (k + 1) // 2) % HOP == HOP - 1
 
     def sum_step(k):
         zb = block_of(k)
         x_copy(k).wait_recv()
         value = summed[zb, xl] + x_in[zb]
-        starts_chain = (k == 0) | (k == 2) | (half - (k + 1) // 2 == sum_skip - 1)
-
-        @pl.when(starts_chain)
-        def _():
-            ring_out[k] = value
-
-        @pl.when(jnp.logical_not(starts_chain))
-        def _():
-            before = jnp.maximum(k - 2, 0)
+        if not starts_chain(k):
+            before = max(k - 2, 0)
             ring_copy(before).wait_recv()
-            ring_out[k] = value + ring_in[before]
-
+            value = value + ring_in[before]
+        ring_out[k] = value
         ring_copy(k).start()
 
-    def block_step_of(k, carry):
-        @pl.when(k < nz)
-        def _():
-            histogram(k)
-
-        @pl.when((k > 0) & (k <= nz))
+    def block_step(k, carry):
+        histogram(k)
+
+        @pl.when(k > 0)
         def _():
             start_x(k - 1)
 
-        @pl.when(k >= LAG)
-        def _():
-            sum_step(k - LAG)
-
-        return carry
-
-    lax.fori_loop(0, nz - 1 + LAG, block_step_of, 0)
+        return carry
+
+    when = {}
+    for k in range(nz - 1):
+        when[k] = 4.2 + 0.79 * k
+        if not starts_chain(k):
+            when[k] = max(when[k], when[max(k - 2, 0)] + 3.1)
+    done = 0
+    for k in sorted(when, key=when.get):
+        count = min(nz, max(int(when[k] / 0.65), k + 2, done))
+        if count > done:
+            lax.fori_loop(done, count, block_step, 0)
+        if count == nz and done < nz:
+            start_x(nz - 1)
+        done = count
+        sum_step(k)
     x_copy(nz - 1).wait_recv()
     total = summed[z, xl] + x_in[z]
-    last_far = 2 * (half - sum_skip)
-    for k in sorted({last_far - 1, last_far, nz - 3, nz - 2}):
-        ring_copy(k).wait_recv()
-        total = total + ring_in[k]
+    for k in range(nz - 1):
+        d = half - (k + 1) // 2
+        if d == 1 or d % HOP == 0:
+            ring_copy(k).wait_recv()
+            total = total + ring_in[k]
     own[...] = total
     dev[:QUARTER] = total[:QUARTER] - total[2 * QUARTER : 2 * QUARTER + 1]
     dev[QUARTER:] = total[QUARTER : 2 * QUARTER] - total[2 * QUARTER + 1 : 2 * QUARTER + 2]
 
-    slot_of = {}
-    blk_sends = []
-
-    def block_copy(src, way, d, to):
-        n = slot_of.setdefault((way, d), len(slot_of))
-        copy = send(src, blocks.at[n], blk_s.at[n], blk_r.at[n], to_ev=along(way * to))
-        copy.start()
-        blk_sends.append(copy)
-
-    def forward(n, src, origin, waiting=False):
+    def relay_copy(r, src):
+        n = 2 * (abs(r) - 1) + (r < 0)
+        return send(
+            src, blocks.at[n], blk_s.at[n], blk_r.at[n], to_ev=along(HOP if r > 0 else -HOP)
+        )
+
+    def direct(r, src, waiting=False):
+        origin = z_at(-HOP * r)
         owner = origin // slots
         slot = lax.rem(origin, slots)
-
-        @pl.when(owner != u)
-        def _():
-            copy = send(src, rows_in.at[slot, u], fwd_s.at[n], rows_r.at[slot, u], to_u=owner)
-            if waiting:
-                copy.wait_send()
-            else:
-                copy.start()
-
-        if not waiting:
-
-            @pl.when(owner == u)
-            def _():
-                rows_in[slot, u] = src[...]
-
-    reach = {1: half, -1: half - 1}
-    for way in (1, -1):
-        if blk_skip <= reach[way]:
-            block_copy(dev, way, blk_skip, blk_skip)
-    for way in (1, -1):
-        block_copy(dev, way, 1, 1)
+        for away in targets[r]:
+            n = HOP * r + away + half - 1
+            copy = send(
+                src, rows_in.at[slot, u], fwd_s.at[n], rows_r.at[slot, u],
+                to_ev=along(away), to_u=owner,
+            )
+            run = copy.wait_send if waiting else copy.start
+            if away:
+                run()
+                continue
+            pl.when(owner != u)(run)
+            if not waiting:
+
+                @pl.when(owner == u)
+                def _():
+                    rows_in[slot, u] = src[...]
+
+    if relays:
+        relay_copy(1, dev).start()
+        relay_copy(-1, dev).start()
 
     def cols_copy(j):
         return send(dev, cols_in.at[u], cols_s.at[j], cols_r.at[u], to_u=lax.rem(u + j, nu))
@@ -363,8 +395,8 @@
         cols_copy(j).start()
         return carry
 
+    direct(0, dev)
     lax.fori_loop(1, nu, start_cols, 0)
-    forward(0, dev, z)
     cols_in[u] = dev[...]
 
     mine = 2 * xl + c
@@ -379,25 +411,16 @@
         spec_copy(i).start()
     spec_in[mine] = own[pl.ds(pl.multiple_of(xl * QUARTER, QUARTER), QUARTER)]
 
-    forwards = []
-
-    def block_step(way, d):
-        n = slot_of[way, d]
-        send(dev, blocks.at[n], blk_s.at[n], blk_r.at[n], to_ev=along(way)).wait_recv()
-        if d + 1 <= reach[way] and d + 1 != blk_skip:
-            block_copy(blocks.at[n], way, d + 1, 1)
-        forwards.append((blocks.at[n], z_at(-way * d)))
-        forward(len(forwards), *forwards[-1])
-
-    near = list(range(1, blk_skip))
-    far = list(range(blk_skip, half + 1))
-    order = near[:1]
-    for i in range(max(len(far), len(near) - 1)):
-        order += far[i : i + 1] + near[i + 1 : i + 2]
-    for d in order:
-        for way in (1, -1):
-            if d <= reach[way]:
-                block_step(way, d)
+    def block_of_relay(r):
+        return blocks.at[2 * (abs(r) - 1) + (r < 0)]
+
+    for r in range(1, relays + 1):
+        for relay in (r, -r):
+            relay_copy(relay, dev).wait_recv()
+            if r < relays:
+                relay_copy(relay + (1 if relay > 0 else -1), block_of_relay(relay)).start()
+        for relay in (r, -r):
+            direct(relay, block_of_relay(relay))
 
     for i in range(3):
         spec_copy(i).wait_recv()
@@ -440,12 +463,23 @@
             pack_out.at[slot], pack_in.at[slot], tail_s.at[1, slot], tail_r.at[1, slot], to_ev=x_ev
         )
 
-    for slot in range(slots):
+    def local_rows(slot):
+        d = lax.rem(z - (u * slots + slot) + nz + half - 1, nz) - (half - 1)
+        relay = jnp.minimum((d + 1 + HOP * nz) // HOP - nz, relays)
+        return d == HOP * relay
+
+    from_below = lax.rem(z - u * slots + nz, nz) <= half
+    for i in range(slots):
+        slot = jnp.where(from_below, slots - 1 - i, i)
 
         def wait_rows(j, carry, slot=slot):
             v = lax.rem(u + j, nu)
-            send(dev, rows_in.at[slot, v], cols_s.at[0], rows_r.at[slot, v], to_u=v).wait_recv()
+            send(dev, rows_in.at[slot, v], cols_s.at[0], rows_r.at[slot, v], to_ev=core_ev).wait_recv()
             return carry
+
+        @pl.when(jnp.logical_not(local_rows(slot)))
+        def _(wait_rows=wait_rows):
+            wait_rows(0, 0)
 
         lax.fori_loop(1, nu, wait_rows, 0)
         rows = jnp.concatenate(
@@ -462,7 +496,8 @@
         prod[slot, 0] = product[:LANES]
         prod[slot, 1] = product[LANES:]
         core_tail(slot).start()
-    for slot in range(slots):
+    for i in range(slots):
+        slot = jnp.where(from_below, slots - 1 - i, i)
         core_tail(slot).wait_recv()
         pack_out[slot] = prod[slot, c, xl_rows] + prod_in[slot, xl_rows]
         x_tail(slot).start()
@@ -478,16 +513,12 @@
 
     lax.fori_loop(0, nz, drain, 0)
 
-    def drain_sums(k, carry):
+    for k in range(nz - 1):
         ring_copy(k).wait_send()
-        return carry
-
-    lax.fori_loop(0, nz - 1, drain_sums, 0)
-    for copy in blk_sends:
-        copy.wait_send()
-    forward(0, dev, z, waiting=True)
-    for n, (src, origin) in enumerate(forwards):
-        forward(n + 1, src, origin, waiting=True)
+    for r in range(-relays, relays + 1):
+        if r:
+            relay_copy(r, dev).wait_send()
+        direct(r, dev, waiting=True)
 
     def drain_cols(j, carry):
         cols_copy(j).wait_send()
@@ -529,14 +560,14 @@
             buf(nz, *block),
             buf(nz - 1, *block), buf(nz - 1, *block),
             buf(*block), buf(*blk),
-            buf(nz - 1, *blk),
+            buf(2 * max(1, nz // 2 // HOP), *blk),
             buf(slots, nu, *blk), buf(nu, *blk),
             buf(4, QUARTER, LANES),
             buf(slots, 2, LANES, 2 * LANES), buf(slots, LANES, 2 * LANES),
             buf(slots, LANES // 2, 2 * LANES), buf(slots, LANES // 2, 2 * LANES),
             dma(nz), dma(nz), dma(nz), dma(nz),
             dma(nz - 1), dma(nz - 1),
-            dma(nz - 1), dma(nz - 1),
+            dma(2 * max(1, nz // 2 // HOP)), dma(2 * max(1, nz // 2 // HOP)),
             dma(nz), dma(slots, nu), dma(nu), dma(nu),
             dma(3), dma(3), dma(2, slots), dma(2, slots),
         ],

time: 79.3 us -> 71.1 us (0.90)
  Pallas kernels: 77.2 us -> 68.9 us
    pallas_call x1, Pallas kernels: 74.1 us -> 65.8 us  [exchange(): pl.pallas_call(functools.partial(exchange_kernel, nz, nu, spec_scale, cov...]
where the time goes in v4:
time: 71.1 us; the launch traced here: 70.9 us
  Pallas kernels  68.9 us (97%)
  local copies, waits for them, and re-layouts  1.27 us (2%)
    pallas_call x1, Pallas kernels, exchange(): pl.pallas_call(functools.partial(exchange_kernel, nz, nu, spec_scale, cov...  65.8 us
    pallas_call x1, Pallas kernels, windows(): pl.pallas_call(windows_kernel, out_shape=(shape((nz, responses.shape[0],...  3.12 us

profile of v4, /device:TPU:5, one launch (start us, length us, event | category | flops | bytes accessed | tf_op | source)
XLA Modules:
  0.0 70.9 jit_solution(1420380951776755719)
XLA Ops:
  0.6 3.1 %windows.1 = (bf16[16,64,1280]{2,1,0:T(8,128)(2,1)S(1)}, s32[16,1,1280]{2,1,0:T(1,128)S(1)}, f32[16,1,1280]{2,1,0:T(1,128)S(1)}, bf16[128,64]{1,0:T(8,128)(2,1)S(1)}, f32[2,16,2,72,128]{4,3,2,1,0:T(8,128)S(1)}) custom-call(bf16[64,16384]{1,0:T(8,128)(2,1)} %resp_hbm.1, s32[128,128]{1,0:T(8,128)} %bitcast.4, bf16[128,128]{1,0:T(8,128)(2,1)} %bitcast.5, ...), custom_call_target="tpu_custom_call" | custom-call | tf_op jit(solution)/shard_map/windows/pallas_call | solution.py:170
  3.8 65.8 %exchange.1 = (f32[64,128]{1,0:T(8,128)S(1)}, f32[64,512]{1,0:T(8,128)S(1)}) custom-call(bf16[16,64,1280]{2,1,0:T(8,128)(2,1)S(1)} %get-tuple-element.9.resp_of, s32[16,1,1280]{2,1,0:T(1,128)S(1)} %get-tuple-element.10.local_of, f32[16,1,1280]{2,1,0:T(1,128)S(1)} %get-tuple-element.11.nominal_of, bf16[128,64]{1,0:T(8,128)(2,1)S(1)} %get-tuple-element.12.throws_t, ...), custom_call_target="tpu_custom_call" | custom-call | tf_op jit(solution)/shard_map/exchange/pallas_call | solution.py:548
  69.6 0.6 copy.8
  70.2 0.7 copy.9

commit v5 on v4

--- a/solution.py
+++ b/solution.py
@@ -9,7 +9,7 @@
 
 LANES = 128
 QUARTER = 32
-BLOCK_ROWS = 72
+BLOCK_ROWS = 66
 CHUNK = 512
 WINDOW = 1280
 HOP = 3
@@ -42,7 +42,7 @@
 def quarter_blocks(sums):
     row = lax.broadcasted_iota(jnp.int32, (8, LANES), 0)
     tail = sums[4 * QUARTER : 4 * QUARTER + 8]
-    central = jnp.where(row == 0, tail[:, :LANES], tail[:, LANES:])
+    central = jnp.where(row == 0, tail[:, :LANES], tail[:, LANES:])[:2]
     for quarter in range(4):
         mine = sums[quarter * QUARTER : (quarter + 1) * QUARTER]
         block = jnp.concatenate([mine[:, :LANES], mine[:, LANES:], central], axis=0)
@@ -235,9 +235,18 @@
             device_id={"ev": to_ev, "uni": to_u}, device_id_type=MESH,
         )
 
+    def still_to_go(d):
+        end = max(d // HOP * HOP, 1)
+        return 3.1 * (d - end) + 2.3 + 0.7 * end
+
+    order = sorted(range(1, half + 1), key=lambda d: -still_to_go(d))
+    away_of = [way * d for d in order for way in (1, -1) if way * d > -half] + [0]
+    place = {d: k for k, d in enumerate(away_of)}
+
     def block_of(k):
-        j = (k + 1) // 2
-        away = jnp.where(lax.rem(k, 2) == 1, half - j, nz - half + j)
+        if isinstance(k, int):
+            return z_at(away_of[k])
+        away = sum(jnp.where(k == i, d % nz, 0) for i, d in enumerate(away_of))
         return lax.rem(z + away, nz)
 
     def tell(to_ev, to_u=u):
@@ -303,23 +312,22 @@
         x_copy(k).start()
 
     def ring_copy(k):
-        d, way = half - (k + 1) // 2, 1 if k % 2 or k == 0 else -1
-        to = d if d == 1 or d % HOP == 0 else 1
-        return send(
-            ring_out.at[k], ring_in.at[k], ring_s.at[k], ring_r.at[k], to_ev=along(way * to)
-        )
-
-    def starts_chain(k):
-        return k in (0, 2) or (half - (k + 1) // 2) % HOP == HOP - 1
+        d = away_of[k]
+        to = d if abs(d) == 1 or d % HOP == 0 else (1 if d > 0 else -1)
+        return send(ring_out.at[k], ring_in.at[k], ring_s.at[k], ring_r.at[k], to_ev=along(to))
+
+    def before(k):
+        d = away_of[k]
+        farther = d + (1 if d > 0 else -1)
+        return place.get(farther) if farther % HOP else None
 
     def sum_step(k):
         zb = block_of(k)
         x_copy(k).wait_recv()
         value = summed[zb, xl] + x_in[zb]
-        if not starts_chain(k):
-            before = max(k - 2, 0)
-            ring_copy(before).wait_recv()
-            value = value + ring_in[before]
+        if before(k) is not None:
+            ring_copy(before(k)).wait_recv()
+            value = value + ring_in[before(k)]
         ring_out[k] = value
         ring_copy(k).start()
 
@@ -333,10 +341,8 @@
         return carry
 
     when = {}
-    for k in range(nz - 1):
-        when[k] = 4.2 + 0.79 * k
-        if not starts_chain(k):
-            when[k] = max(when[k], when[max(k - 2, 0)] + 3.1)
+    for k in sorted(range(nz - 1), key=lambda k: -abs(away_of[k])):
+        when[k] = max(4.2 + 0.75 * k, when.get(before(k), 0.0) + 3.1)
     done = 0
     for k in sorted(when, key=when.get):
         count = min(nz, max(int(when[k] / 0.65), k + 2, done))
@@ -349,8 +355,7 @@
     x_copy(nz - 1).wait_recv()
     total = summed[z, xl] + x_in[z]
     for k in range(nz - 1):
-        d = half - (k + 1) // 2
-        if d == 1 or d % HOP == 0:
+        if abs(away_of[k]) == 1 or away_of[k] % HOP == 0:
             ring_copy(k).wait_recv()
             total = total + ring_in[k]
     own[...] = total

time: 71.1 us -> 68.9 us (0.969)
  Pallas kernels: 68.9 us -> 66.8 us
    pallas_call x1, Pallas kernels: 65.8 us -> 63.7 us  [exchange(): pl.pallas_call(functools.partial(exchange_kernel, nz, nu, spec_scale, cov...]
where the time goes in v5:
time: 68.9 us; the launch traced here: 68.7 us
  Pallas kernels  66.8 us (97%)
  local copies, waits for them, and re-layouts  1.27 us (2%)
    pallas_call x1, Pallas kernels, exchange(): pl.pallas_call(functools.partial(exchange_kernel, nz, nu, spec_scale, cov...  63.7 us
    pallas_call x1, Pallas kernels, windows(): pl.pallas_call(windows_kernel, out_shape=(shape((nz, responses.shape[0],...  3.12 us

profile of v5, /device:TPU:5, one launch (start us, length us, event | category | flops | bytes accessed | tf_op | source)
XLA Modules:
  0.0 68.7 jit_solution(15692208930181857575)
XLA Ops:
  0.6 3.1 %windows.1 = (bf16[16,64,1280]{2,1,0:T(8,128)(2,1)S(1)}, s32[16,1,1280]{2,1,0:T(1,128)S(1)}, f32[16,1,1280]{2,1,0:T(1,128)S(1)}, bf16[128,64]{1,0:T(8,128)(2,1)S(1)}, f32[2,16,2,66,128]{4,3,2,1,0:T(8,128)S(1)}) custom-call(bf16[64,16384]{1,0:T(8,128)(2,1)} %resp_hbm.1, s32[128,128]{1,0:T(8,128)} %bitcast.4, bf16[128,128]{1,0:T(8,128)(2,1)} %bitcast.5, ...), custom_call_target="tpu_custom_call" | custom-call | tf_op jit(solution)/shard_map/windows/pallas_call | solution.py:170
  3.8 63.7 %exchange.1 = (f32[64,128]{1,0:T(8,128)S(1)}, f32[64,512]{1,0:T(8,128)S(1)}) custom-call(bf16[16,64,1280]{2,1,0:T(8,128)(2,1)S(1)} %get-tuple-element.9.resp_of, s32[16,1,1280]{2,1,0:T(1,128)S(1)} %get-tuple-element.10.local_of, f32[16,1,1280]{2,1,0:T(1,128)S(1)} %get-tuple-element.11.nominal_of, bf16[128,64]{1,0:T(8,128)(2,1)S(1)} %get-tuple-element.12.throws_t, ...), custom_call_target="tpu_custom_call" | custom-call | tf_op jit(solution)/shard_map/exchange/pallas_call | solution.py:553
  67.5 0.6 copy.8
  68.1 0.7 copy.9

commit v6 on v5

--- a/solution.py
+++ b/solution.py
@@ -334,9 +334,9 @@
     def block_step(k, carry):
         histogram(k)
 
-        @pl.when(k > 0)
+        @pl.when(k > 1)
         def _():
-            start_x(k - 1)
+            start_x(k - 2)
 
         return carry
 
@@ -345,10 +345,11 @@
         when[k] = max(4.2 + 0.75 * k, when.get(before(k), 0.0) + 3.1)
     done = 0
     for k in sorted(when, key=when.get):
-        count = min(nz, max(int(when[k] / 0.65), k + 2, done))
+        count = min(nz, max(int(when[k] / 0.65), k + 3, done))
         if count > done:
             lax.fori_loop(done, count, block_step, 0)
         if count == nz and done < nz:
+            start_x(nz - 2)
             start_x(nz - 1)
         done = count
         sum_step(k)
@@ -372,7 +373,7 @@
         origin = z_at(-HOP * r)
         owner = origin // slots
         slot = lax.rem(origin, slots)
-        for away in targets[r]:
+        for away in sorted(targets[r], key=abs, reverse=True):
             n = HOP * r + away + half - 1
             copy = send(
                 src, rows_in.at[slot, u], fwd_s.at[n], rows_r.at[slot, u],
@@ -424,8 +425,11 @@
             relay_copy(relay, dev).wait_recv()
             if r < relays:
                 relay_copy(relay + (1 if relay > 0 else -1), block_of_relay(relay)).start()
-        for relay in (r, -r):
-            direct(relay, block_of_relay(relay))
+            else:
+                direct(relay, block_of_relay(relay))
+        if r < relays:
+            for relay in (r, -r):
+                direct(relay, block_of_relay(relay))
 
     for i in range(3):
         spec_copy(i).wait_recv()
@@ -457,15 +461,16 @@
     xl_rows = pl.ds(pl.multiple_of((1 - xl) * (LANES // 2), LANES // 2), LANES // 2)
     my_rows = pl.ds(pl.multiple_of(xl * (LANES // 2), LANES // 2), LANES // 2)
 
-    def core_tail(slot):
+    def core_tail(slot, h):
         return send(
-            prod.at[slot, 1 - c], prod_in.at[slot], tail_s.at[0, slot], tail_r.at[0, slot],
-            to_ev=core_ev,
-        )
-
-    def x_tail(slot):
+            prod.at[slot, h, 1 - c], prod_in.at[slot, h],
+            tail_s.at[0, slot, h], tail_r.at[0, slot, h], to_ev=core_ev,
+        )
+
+    def x_tail(slot, h):
         return send(
-            pack_out.at[slot], pack_in.at[slot], tail_s.at[1, slot], tail_r.at[1, slot], to_ev=x_ev
+            pack_out.at[slot, h], pack_in.at[slot, h],
+            tail_s.at[1, slot, h], tail_r.at[1, slot, h], to_ev=x_ev,
         )
 
     def local_rows(slot):
@@ -487,29 +492,27 @@
             wait_rows(0, 0)
 
         lax.fori_loop(1, nu, wait_rows, 0)
-        rows = jnp.concatenate(
-            [
-                rows_in[slot, :, :QUARTER].reshape(depth, LANES),
-                rows_in[slot, :, QUARTER:].reshape(depth, LANES),
-            ],
-            axis=1,
-        )
-        rows_hi = rows.astype(bf16)
-        rows_lo = (rows - rows_hi.astype(F32)).astype(bf16)
-        rows_all = jnp.concatenate([rows_hi, rows_lo, rows_hi], axis=0)
-        product = jnp.dot(cols_all, rows_all, preferred_element_type=F32)
-        prod[slot, 0] = product[:LANES]
-        prod[slot, 1] = product[LANES:]
-        core_tail(slot).start()
+        for h in range(2):
+            rows = rows_in[slot, :, h * QUARTER : (h + 1) * QUARTER].reshape(depth, LANES)
+            rows_hi = rows.astype(bf16)
+            rows_lo = (rows - rows_hi.astype(F32)).astype(bf16)
+            rows_all = jnp.concatenate([rows_hi, rows_lo, rows_hi], axis=0)
+            product = jnp.dot(cols_all, rows_all, preferred_element_type=F32)
+            prod[slot, h, 0] = product[:LANES]
+            prod[slot, h, 1] = product[LANES:]
+            core_tail(slot, h).start()
     for i in range(slots):
         slot = jnp.where(from_below, slots - 1 - i, i)
-        core_tail(slot).wait_recv()
-        pack_out[slot] = prod[slot, c, xl_rows] + prod_in[slot, xl_rows]
-        x_tail(slot).start()
+        for h in range(2):
+            core_tail(slot, h).wait_recv()
+            pack_out[slot, h] = prod[slot, h, c, xl_rows] + prod_in[slot, h, xl_rows]
+            x_tail(slot, h).start()
     for slot in range(slots):
-        x_tail(slot).wait_recv()
-        keep = prod[slot, c, my_rows] + prod_in[slot, my_rows]
-        cov[:, slot * 2 * LANES : (slot + 1) * 2 * LANES] = (keep + pack_in[slot]) * cov_scale
+        for h in range(2):
+            x_tail(slot, h).wait_recv()
+            keep = prod[slot, h, c, my_rows] + prod_in[slot, h, my_rows]
+            at = (2 * slot + h) * LANES
+            cov[:, at : at + LANES] = (keep + pack_in[slot, h]) * cov_scale
 
     def drain(k, carry):
         core_copy(k).wait_send()
@@ -533,8 +536,9 @@
     for i in range(3):
         spec_copy(i).wait_send()
     for slot in range(slots):
-        core_tail(slot).wait_send()
-        x_tail(slot).wait_send()
+        for h in range(2):
+            core_tail(slot, h).wait_send()
+            x_tail(slot, h).wait_send()
 
 
 def exchange(taken, nz, nu, spec_scale, cov_scale):
@@ -568,13 +572,13 @@
             buf(2 * max(1, nz // 2 // HOP), *blk),
             buf(slots, nu, *blk), buf(nu, *blk),
             buf(4, QUARTER, LANES),
-            buf(slots, 2, LANES, 2 * LANES), buf(slots, LANES, 2 * LANES),
-            buf(slots, LANES // 2, 2 * LANES), buf(slots, LANES // 2, 2 * LANES),
+            buf(slots, 2, 2, LANES, LANES), buf(slots, 2, LANES, LANES),
+            buf(slots, 2, LANES // 2, LANES), buf(slots, 2, LANES // 2, LANES),
             dma(nz), dma(nz), dma(nz), dma(nz),
             dma(nz - 1), dma(nz - 1),
             dma(2 * max(1, nz // 2 // HOP)), dma(2 * max(1, nz // 2 // HOP)),
             dma(nz), dma(slots, nu), dma(nu), dma(nu),
-            dma(3), dma(3), dma(2, slots), dma(2, slots),
+            dma(3), dma(3), dma(2, slots, 2), dma(2, slots, 2),
         ],
         compiler_params=pltpu.CompilerParams(
             collective_id=0, has_side_effects=True, vmem_limit_bytes=VMEM_GRANT

time: 68.9 us -> 67.8 us (0.984)
  the two profiles are of different devices: /device:TPU:5 before, /device:TPU:24 now
where the time goes in v6:
time: 67.8 us; the launch traced here: 67.6 us
  Pallas kernels  65.6 us (97%)
  local copies, waits for them, and re-layouts  1.27 us (2%)
    pallas_call x1, Pallas kernels, exchange(): pl.pallas_call(functools.partial(exchange_kernel, nz, nu, spec_scale, cov...  62.5 us
    pallas_call x1, Pallas kernels, windows(): pl.pallas_call(windows_kernel, out_shape=(shape((nz, responses.shape[0],...  3.12 us

profile of v6, /device:TPU:24, one launch (start us, length us, event | category | flops | bytes accessed | tf_op | source)
XLA Modules:
  0.0 67.6 jit_solution(2186562216155171527)
XLA Ops:
  0.6 3.1 %windows.1 = (bf16[16,64,1280]{2,1,0:T(8,128)(2,1)S(1)}, s32[16,1,1280]{2,1,0:T(1,128)S(1)}, f32[16,1,1280]{2,1,0:T(1,128)S(1)}, bf16[128,64]{1,0:T(8,128)(2,1)S(1)}, f32[2,16,2,66,128]{4,3,2,1,0:T(8,128)S(1)}) custom-call(bf16[64,16384]{1,0:T(8,128)(2,1)} %resp_hbm.1, s32[128,128]{1,0:T(8,128)} %bitcast.4, bf16[128,128]{1,0:T(8,128)(2,1)} %bitcast.5, ...), custom_call_target="tpu_custom_call" | custom-call | tf_op jit(solution)/shard_map/windows/pallas_call | solution.py:170
  3.8 62.5 %exchange.1 = (f32[64,128]{1,0:T(8,128)S(1)}, f32[64,512]{1,0:T(8,128)S(1)}) custom-call(bf16[16,64,1280]{2,1,0:T(8,128)(2,1)S(1)} %get-tuple-element.9.resp_of, s32[16,1,1280]{2,1,0:T(1,128)S(1)} %get-tuple-element.10.local_of, f32[16,1,1280]{2,1,0:T(1,128)S(1)} %get-tuple-element.11.nominal_of, bf16[128,64]{1,0:T(8,128)(2,1)S(1)} %get-tuple-element.12.throws_t, ...), custom_call_target="tpu_custom_call" | custom-call | tf_op jit(solution)/shard_map/exchange/pallas_call | solution.py:557
  66.3 0.6 copy.8
  66.9 0.7 copy.9
